TPU v7x, 32 devices: a whole 2x2x4 slice. The times are simulated.
32 devices in a mesh: dp: 4 (over z), shard: 8 (over y, x, core).
Axes of the slice: x: 2, y: 2, z: 4, core: 2. Of those that a mesh axis runs over, the one named last changes fastest.
Arguments:
- attention_grad: float32 [4, 3968, 3968], P('dp', 'shard'), may hold values from -127 to 127
- attention_error: float32 [4, 3968, 3968], P('dp', 'shard'), may hold values from -64 to 64
- attention_warm: float32 [32, 3968], replicated, may hold values from -6 to 6
- feedforward_grad: float32 [4, 7936, 2048], P('dp', 'shard'), may hold values from -127 to 127
- feedforward_error: float32 [4, 7936, 2048], P('dp', 'shard'), may hold values from -64 to 64
- feedforward_warm: float32 [32, 2048], replicated, may hold values from -6 to 6
Outputs:
- attention_carry: float32 [4, 3968, 3968], P('dp', 'shard')
- feedforward_carry: float32 [4, 7936, 2048], P('dp', 'shard')
- attention_basis: float32 [32, 3968], replicated
- feedforward_basis: float32 [32, 2048], replicated
All inputs are finite; a program needn't handle non-finite values.
Results may differ from a plain program's by a relative error of at most 0.00025.
Values sent between devices are 32-bit elements; how exact they have to be, the bound alone decides.
No kernel may reach another device: no remote copies, remote signals or barrier semaphores. Data moves between devices by JAX's collectives and lax.ppermute only.
A program may use at most 128 MiB of HBM per device.

v0:
```python
import jax
import jax.numpy as jnp
from jax import lax
from jax.sharding import PartitionSpec as P

ITERS = 2


highest = lax.Precision.HIGHEST


def left_product(matrix, factor):
    return lax.dot_general(
        matrix,
        factor,
        (((1,), (1,)), ((), ())),
        precision=highest,
        preferred_element_type=jnp.float32,
    )


def right_product(basis, matrix):
    return lax.dot_general(
        basis,
        matrix,
        (((0,), (0,)), ((), ())),
        precision=highest,
        preferred_element_type=jnp.float32,
    )


def orthonormal(left, gram):
    lower = jnp.linalg.cholesky(gram)
    return jax.scipy.linalg.solve_triangular(lower, left.T, lower=True).T


def shards(
    attention_grad,
    attention_error,
    attention_warm,
    feedforward_grad,
    feedforward_error,
    feedforward_warm,
):
    first_matrix = attention_grad[0] + attention_error[0]
    second_matrix = feedforward_grad[0] + feedforward_error[0]
    first_factor = attention_warm
    second_factor = feedforward_warm
    replicas = lax.axis_size("dp")
    first_basis = None
    second_basis = None
    for sweep in range(ITERS):
        first_left, second_left = lax.psum(
            (left_product(first_matrix, first_factor), left_product(second_matrix, second_factor)),
            "dp",
        )
        first_gram, second_gram = lax.psum(
            (right_product(first_left, first_left), right_product(second_left, second_left)),
            "shard",
        )
        first_basis = orthonormal(first_left, first_gram)
        second_basis = orthonormal(second_left, second_gram)
        first_terms = right_product(first_basis, first_matrix)
        second_terms = right_product(second_basis, second_matrix)
        first_share, second_share = (
            lax.psum_scatter(first_terms, "shard", scatter_dimension=1, tiled=True),
            lax.psum_scatter(second_terms, "shard", scatter_dimension=1, tiled=True),
        )
        first_share, second_share = lax.psum((first_share, second_share), "dp")
        first_factor, second_factor = (
            lax.all_gather(first_share / replicas, "shard", axis=1, tiled=True),
            lax.all_gather(second_share / replicas, "shard", axis=1, tiled=True),
        )
    first_carry = first_matrix - jnp.dot(
        first_basis, first_factor, precision=highest, preferred_element_type=jnp.float32
    )
    second_carry = second_matrix - jnp.dot(
        second_basis, second_factor, precision=highest, preferred_element_type=jnp.float32
    )
    return (first_carry[None], second_carry[None], first_factor, second_factor)


def solution(mesh):
    placed = (
        P("dp", "shard", None),
        P("dp", "shard", None),
        P(),
        P("dp", "shard", None),
        P("dp", "shard", None),
        P(),
    )
    return jax.shard_map(
        shards,
        mesh=mesh,
        in_specs=placed,
        out_specs=(P("dp", "shard", None), P("dp", "shard", None), P(), P()),
        check_vma=False,
    )
```

profile of v0, /device:TPU:0, one launch (start us, length us, event | category | flops | bytes accessed | tf_op | source)
XLA Modules:
  0.0 494.9 jit_solution(4828861286687608190)
XLA Ops:
  7.2 11.6 %add.57 = f32[1,992,2048]{2,1,0:T(8,128)} add(f32[1,992,2048]{2,1,0:T(8,128)} %param.14, f32[1,992,2048]{2,1,0:T(8,128)} %param.15) | non-fusion elementwise | flops 2031616 | bytes 24379392 | tf_op jit(solution)/shard_map/add | solution.py:46
  18.8 10.0 %fusion.6 = f32[992,32]{0,1:T(8,128)} fusion(f32[32,2048]{1,0:T(8,128)S(1)} %copy-done.7, f32[1,992,2048]{2,1,0:T(8,128)} %add.57), kind=kOutput, calls=%fused_computation.7 | convolution fusion | flops 780140544 | bytes 8515584 | tf_op jit(solution)/shard_map/dot_general | solution.py:13
  45.2 22.1 %psum.84 = f32[496,32]{0,1:T(8,128)S(1)} all-reduce(f32[496,32]{0,1:T(8,128)S(1)} %fusion.15), channel_id=1, replica_groups=mesh['dp'=4,'shard'=8] {'dp'}, use_global_device_ids=true, to_apply=%region_0.0 | all-reduce | flops 15872 | bytes 126976 | tf_op jit(solution)/shard_map/psum | solution.py:53
  68.9 22.4 %all-reduce.1 = (f32[32,32]{0,1:T(8,128)S(1)}, f32[32,32]{0,1:T(8,128)S(1)}) all-reduce(f32[32,32]{0,1:T(8,128)S(1)} %fusion.46, f32[32,32]{0,1:T(8,128)S(1)} %fusion.48), channel_id=1, replica_groups=mesh['dp'=4,'shard'=8] {'shard'}, use_global_device_ids=true, to_apply=%region_1.0 | all-reduce | flops 2048 | bytes 16384 | tf_op jit(solution)/shard_map/psum | solution.py:57
  98.4 16.6 %fusion.18 = f32[3968,32]{1,0:T(8,128)} fusion(f32[32,496]{1,0:T(8,128)S(1)} %fusion.30, f32[1,496,3968]{2,1,0:T(8,128)} %copy-done.2), kind=kOutput, calls=%fused_computation.20 | convolution fusion | flops 755761152 | bytes 8443904
  122.1 8.1 %fusion.4 = f32[32,2048]{1,0:T(8,128)} fusion(f32[32,992]{1,0:T(8,128)S(1)} %fusion.26, f32[1,992,2048]{2,1,0:T(8,128)} %add.57), kind=kOutput, calls=%fused_computation.5 | convolution fusion | flops 780140544 | bytes 8515584 | tf_op jit(solution)/shard_map/dot_general | solution.py:23
  130.2 23.5 %reduce-scatter.13.cloned.1.call-done = f32[496,32]{1,0:T(8,128)} async-done(((f32[3968,32]{1,0:T(8,128)}), f32[496,32]{1,0:T(8,128)}) %reduce-scatter.13.cloned.1.call-update) | async-done | bytes 63504
  154.7 19.8 %psum.86 = f32[32,496]{1,0:T(8,128)S(1)} all-reduce(f32[32,496]{1,0:T(8,128)S(1)} %copy.43), channel_id=1, replica_groups=mesh['dp'=4,'shard'=8] {'dp'}, use_global_device_ids=true, to_apply=%region_5.8 | all-reduce | flops 15872 | bytes 126976 | tf_op jit(solution)/shard_map/psum | solution.py:69
  174.5 10.2 %all-gather = f32[8,496,32]{1,2,0:T(8,128)S(1)} all-gather(f32[1,496,32]{1,2,0:T(8,128)S(1)} %multiply_bitcast_fusion.1), channel_id=1, replica_groups=mesh['dp'=4,'shard'=8] {'shard'}, dimensions={0}, use_global_device_ids=true | all-gather | bytes 571392 | tf_op jit(solution)/shard_map/all_gather | solution.py:71
  185.4 9.9 %fusion.11 = f32[496,32]{0,1:T(8,128)} fusion(f32[3968,32]{0,1:T(8,128)S(1)} %reshape.22, f32[1,496,3968]{2,1,0:T(8,128)} %copy-done.2), kind=kOutput, calls=%fused_computation.13 | convolution fusion | flops 755761152 | bytes 8443904 | tf_op jit(solution)/shard_map/dot_general | solution.py:13
  195.4 33.0 %all-reduce.15.cloned.1.call-done = (f32[496,32]{0,1:T(8,128)}, f32[32,256]{1,0:T(8,128)}) async-done(((f32[496,32]{0,1:T(8,128)}, f32[32,256]{1,0:T(8,128)}), (f32[496,32]{0,1:T(8,128)}, f32[32,256]{1,0:T(8,128)})) %all-reduce.15.cloned.1.call-update) | async-done | bytes 96272 | tf_op jit(solution)/shard_map/psum | solution.py:53
  229.2 9.2 %all_gather.14 = f32[32,2048]{1,0:T(8,128)S(1)} all-gather(f32[32,256]{1,0:T(8,128)S(1)} %broadcast_multiply_fusion.1), channel_id=1, replica_groups=mesh['dp'=4,'shard'=8] {'shard'}, dimensions={1}, use_global_device_ids=true | all-gather | bytes 294912 | tf_op jit(solution)/shard_map/all_gather | solution.py:72
  238.5 10.0 %fusion.2 = f32[992,32]{0,1:T(8,128)} fusion(f32[32,2048]{1,0:T(8,128)S(1)} %all_gather.14, f32[1,992,2048]{2,1,0:T(8,128)} %add.57), kind=kOutput, calls=%fused_computation.3 | convolution fusion | flops 780140544 | bytes 8515584 | tf_op jit(solution)/shard_map/dot_general | solution.py:13
  248.7 33.4 %all-reduce.11.cloned.1.call-done = f32[992,32]{0,1:T(8,128)} async-done(((f32[992,32]{0,1:T(8,128)}), f32[992,32]{0,1:T(8,128)}) %all-reduce.11.cloned.1.call-update) | async-done | bytes 126992 | tf_op jit(solution)/shard_map/psum | solution.py:53
  283.5 22.6 %all-reduce = (f32[32,32]{0,1:T(8,128)S(1)}, f32[32,32]{0,1:T(8,128)S(1)}) all-reduce(f32[32,32]{0,1:T(8,128)S(1)} %fusion.47, f32[32,32]{0,1:T(8,128)S(1)} %fusion.49), channel_id=1, replica_groups=mesh['dp'=4,'shard'=8] {'shard'}, use_global_device_ids=true, to_apply=%region_7.10 | all-reduce | flops 2048 | bytes 16384 | tf_op jit(solution)/shard_map/psum | solution.py:57
  313.2 16.6 %fusion.21 = f32[3968,32]{1,0:T(8,128)} fusion(f32[32,496]{1,0:T(8,128)S(1)} %fusion.28, f32[1,496,3968]{2,1,0:T(8,128)} %copy-done.2), kind=kOutput, calls=%fused_computation.21 | convolution fusion | flops 755761152 | bytes 8443904
  336.9 8.1 %fusion = f32[32,2048]{1,0:T(8,128)} fusion(f32[32,992]{1,0:T(8,128)S(1)} %fusion.24, f32[1,992,2048]{2,1,0:T(8,128)} %add.57), kind=kOutput, calls=%fused_computation.1 | convolution fusion | flops 780140544 | bytes 8515584 | tf_op jit(solution)/shard_map/dot_general | solution.py:23
  345.1 24.4 %reduce-scatter.15.cloned.1.call-done = f32[496,32]{1,0:T(8,128)} async-done(((f32[3968,32]{1,0:T(8,128)}), f32[496,32]{1,0:T(8,128)}) %reduce-scatter.15.cloned.1.call-update) | async-done | bytes 63504
  371.2 35.6 %reduce-scatter.11.cloned.1.call-done = f32[32,256]{1,0:T(8,128)} async-done(((f32[32,2048]{1,0:T(8,128)}), f32[32,256]{1,0:T(8,128)}) %reduce-scatter.11.cloned.1.call-update) | async-done | bytes 32784 | tf_op jit(solution)/shard_map/reduce_scatter | solution.py:67
  406.8 37.4 %all-reduce.13.cloned.1.call-done = (f32[32,496]{1,0:T(8,128)}, f32[32,256]{1,0:T(8,128)}) async-done(((f32[32,496]{1,0:T(8,128)}, f32[32,256]{1,0:T(8,128)}), (f32[32,496]{1,0:T(8,128)}, f32[32,256]{1,0:T(8,128)})) %all-reduce.13.cloned.1.call-update) | async-done | bytes 96272 | tf_op jit(solution)/shard_map/psum | solution.py:69
  445.0 9.5 %all_gather.15 = f32[32,2048]{1,0:T(8,128)S(1)} all-gather(f32[32,256]{1,0:T(8,128)S(1)} %broadcast_multiply_fusion), channel_id=1, replica_groups=mesh['dp'=4,'shard'=8] {'shard'}, dimensions={1}, use_global_device_ids=true | all-gather | bytes 294912 | tf_op jit(solution)/shard_map/all_gather | solution.py:72
  454.5 10.9 %fusion.8 = f32[1,992,2048]{2,1,0:T(8,128)} fusion(f32[1,992,2048]{2,1,0:T(8,128)} %add.57, f32[32,992]{1,0:T(8,128)S(1)} %fusion.24, f32[32,2048]{1,0:T(8,128)S(1)} %all_gather.15), kind=kOutput, calls=%fused_computation.9 | convolution fusion | flops 782172160 | bytes 16642048 | tf_op jit(solution)/shard_map/dot_general | solution.py:77
  465.5 9.8 %all-gather.1 = f32[8,496,32]{1,2,0:T(8,128)S(1)} all-gather(f32[1,496,32]{1,2,0:T(8,128)S(1)} %multiply_bitcast_fusion), channel_id=1, replica_groups=mesh['dp'=4,'shard'=8] {'shard'}, dimensions={0}, use_global_device_ids=true | all-gather | bytes 571392 | tf_op jit(solution)/shard_map/all_gather | solution.py:71
  475.9 11.0 %fusion.17 = f32[1,496,3968]{2,1,0:T(8,128)} fusion(f32[1,496,3968]{2,1,0:T(8,128)} %copy-done.2, f32[32,496]{1,0:T(8,128)S(1)} %fusion.28, f32[3968,32]{0,1:T(8,128)S(1)} %reshape.24), kind=kOutput, calls=%fused_computation.19 | convolution fusion | flops 757729280 | bytes 16316416 | tf_op jit(solution)/shard_map/dot_general | solution.py:74
  (84 shorter events, 54.3 us)
Async XLA Ops:
  7.2 31.2 %copy-start = (f32[32,3968]{1,0:T(8,128)S(1)}, f32[32,3968]{1,0:T(8,128)}, u32[]{:S(2)}) copy-start(f32[32,3968]{1,0:T(8,128)} %param.13) | copy-start | bytes 1523716
  7.2 11.7 %copy-start.7 = (f32[32,2048]{1,0:T(8,128)S(1)}, f32[32,2048]{1,0:T(8,128)}, u32[]{:S(2)}) copy-start(f32[32,2048]{1,0:T(8,128)} %param.16) | copy-start | bytes 786436
  7.2 60.4 %all-reduce.9.cloned.1.call-start = ((), (), s32[]{:S(2)}) async-start(), calls=%async_computation.4 | async-start | bytes 262144 | tf_op jit(solution)/shard_map/psum | solution.py:53
  28.8 124.9 %reduce-scatter.13.cloned.1.call-start = ((), (), s32[]{:S(2)}) async-start(), calls=%async_computation.8 | async-start | bytes 2285568
  35.1 3.2 copy-start.2
  67.6 54.2 %copy-start.4 = (f32[992,32]{0,1:T(8,128)S(1)}, f32[992,32]{0,1:T(8,128)}, u32[]{:S(2)}) copy-start(f32[992,32]{0,1:T(8,128)} %all-reduce.9.cloned.1.call-done) | copy-start | bytes 380932
  115.0 80.3 %reduce-scatter.9.cloned.1.call-start = ((), (), s32[]{:S(2)}) async-start(), calls=%async_computation.5 | async-start | bytes 294912 | tf_op jit(solution)/shard_map/reduce_scatter | solution.py:67
  130.2 98.2 %all-reduce.15.cloned.1.call-start = ((), (), s32[]{:S(2)}) async-start(), calls=%async_computation.11 | async-start | bytes 196608 | tf_op jit(solution)/shard_map/psum | solution.py:53
  195.4 86.8 %all-reduce.11.cloned.1.call-start = ((), (), s32[]{:S(2)}) async-start(), calls=%async_computation.6 | async-start | bytes 262144 | tf_op jit(solution)/shard_map/psum | solution.py:53
  228.4 20.1 %copy-start.6 = (f32[496,32]{0,1:T(8,128)S(1)}, f32[496,32]{0,1:T(8,128)}, u32[]{:S(2)}) copy-start(f32[496,32]{0,1:T(8,128)} %get-tuple-element.13) | copy-start | bytes 190468
  248.4 121.0 %reduce-scatter.15.cloned.1.call-start = ((), (), s32[]{:S(2)}) async-start(), calls=%async_computation.9 | async-start | bytes 2285568
  282.1 54.4 %copy-start.5 = (f32[992,32]{0,1:T(8,128)S(1)}, f32[992,32]{0,1:T(8,128)}, u32[]{:S(2)}) copy-start(f32[992,32]{0,1:T(8,128)} %all-reduce.11.cloned.1.call-done) | copy-start | bytes 380932
  329.7 77.1 %reduce-scatter.11.cloned.1.call-start = ((), (), s32[]{:S(2)}) async-start(), calls=%async_computation.7 | async-start | bytes 294912 | tf_op jit(solution)/shard_map/reduce_scatter | solution.py:67
  345.0 99.3 %all-reduce.13.cloned.1.call-start = ((), (), s32[]{:S(2)}) async-start(), calls=%async_computation.10 | async-start | bytes 196608 | tf_op jit(solution)/shard_map/psum | solution.py:69
  454.5 10.9 %copy-start.8 = (f32[32,496]{1,0:T(8,128)S(1)}, f32[32,496]{1,0:T(8,128)}, u32[]{:S(2)}) copy-start(f32[32,496]{1,0:T(8,128)} %get-tuple-element.11) | copy-start | bytes 190468
  475.6 12.0 %copy-start.1 = (f32[32,3968]{1,0:T(8,128)S(1)}, f32[32,3968]{1,0:T(8,128)}, u32[]{:S(2)}) copy-start(f32[32,3968]{1,0:T(8,128)} %param.13) | copy-start | bytes 1523716
  475.9 11.0 %copy-start.3 = (f32[3968,32]{0,1:T(8,128)}, f32[3968,32]{0,1:T(8,128)S(1)}, u32[]{:S(2)}) copy-start(f32[3968,32]{0,1:T(8,128)S(1)} %reshape.24) | copy-start | bytes 1523716
Sparse Core Ops, SparseCore 0:
  29.0 37.3 all-reduce.8
  115.1 38.5 reduce-scatter.12
  157.3 33.7 reduce-scatter.8
  195.5 32.8 all-reduce.14
  248.6 33.5 all-reduce.10
  329.9 39.5 reduce-scatter.14
  373.1 33.6 reduce-scatter.10
  409.8 34.4 all-reduce.12
where the time goes:
time: 504 us; the launch traced here: 495 us
  waiting for transfers between devices  188 us (37%)
  blocking collectives  126 us (25%)
  matrix products  112 us (22%)
  other arithmetic  46.2 us (9%)
  between operations  14.8 us (3%)
  local copies, waits for them, and re-layouts  8.22 us (2%)
    psum x3, waiting for transfers between devices, shards(): lax.psum((left_product(first_matrix, first_factor), left_product(second_m...  66.5 us
    unnamed x10, waiting for transfers between devices  48 us
    psum x2, blocking collectives, shards(): lax.psum((right_product(first_left, first_left), right_product(second_lef...  45 us
    psum x1, waiting for transfers between devices, shards(): first_share, second_share = lax.psum((first_share, second_share), 'dp')  37.4 us
    dot_general x4, matrix products, left_product(): lax.dot_general(matrix, factor, (((1,), (1,)), ((), ())), precision=highe...  36.7 us
    reduce_scatter x2, waiting for transfers between devices, shards(): lax.psum_scatter(second_terms, 'shard', scatter_dimension=1, tiled=True)  35.6 us
    unnamed x2, matrix products  33.1 us
    psum x1, blocking collectives, shards(): lax.psum((left_product(first_matrix, first_factor), left_product(second_m...  22.1 us
  transfers between devices with their start and end apart: 8, of which 6 were waited for; matrix products, arithmetic and copies ran while one was open for 12% of the time, Pallas kernels for 0%

commit v1 on v0

v1 whole, which is shorter than its diff:
```python
import functools

import jax
import jax.numpy as jnp
from jax import lax
from jax.experimental import pallas as pl
from jax.experimental.pallas import tpu as pltpu
from jax.sharding import PartitionSpec as P

ITERS = 2
LANES = 128
DEPTH = 3
MIB = 1 << 20

highest = lax.Precision.HIGHEST
NT = (((1,), (1,)), ((), ()))
NN = (((1,), (0,)), ((), ()))
VMEM = pl.BlockSpec(memory_space=pltpu.VMEM)
ANY = pl.BlockSpec(memory_space=pl.ANY)
HBM = pl.BlockSpec(memory_space=pltpu.HBM)


def dot(a, b, dims):
    return lax.dot_general(a, b, dims, preferred_element_type=jnp.float32)


def dot32(a, b, dims):
    return lax.dot_general(a, b, dims, precision=highest, preferred_element_type=jnp.float32)


def pad(n):
    return -(-n // LANES) * LANES


def split(x):
    high = x.astype(jnp.bfloat16)
    low = (x - high.astype(jnp.float32)).astype(jnp.bfloat16)
    return high, low


def stacked(x):
    high, low = split(x)
    return jnp.concatenate([high, low], axis=0)


def tree(terms):
    terms = list(terms)
    while len(terms) > 1:
        half = len(terms) // 2
        terms = [terms[k] + terms[k + half] for k in range(half)]
    return terms[0]


def three(pair, high, low, dims):
    rank = pair.shape[0] // 2
    first = dot(pair, high, dims)
    return first[:rank] + first[rank:] + dot(pair[:rank], low, dims)


class Plan:
    def __init__(self, rows, cols, rank, shards):
        self.rows, self.cols, self.rank, self.shards = rows, cols, rank, shards
        self.half = shards // 2
        self.row_at = (0, pad(rows[0]))
        self.row_all = pad(rows[0]) + pad(rows[1])
        self.part = tuple(pad(-(-c // shards)) for c in cols)
        self.part_at = (0, self.part[0])
        self.share = sum(self.part)
        self.padded = tuple(p * shards for p in self.part)

    def row_span(self, m):
        return slice(self.row_at[m], self.row_at[m] + pad(self.rows[m]))

    def part_span(self, m):
        return slice(self.part_at[m], self.part_at[m] + self.part[m])

    def columns(self, m, chunk):
        return pl.ds(pl.multiple_of(chunk * self.part[m], LANES), self.part[m])


def params(limit):
    return pltpu.CompilerParams(vmem_limit_bytes=int(limit * MIB))


def cost(us):
    return pl.CostEstimate(flops=0, transcendentals=0, bytes_accessed=int(us * 3.0e6))


def chunk_of(slot):
    return lax.bitwise_xor(jnp.int32(slot), lax.axis_index("shard"))


def blank(plan, m, high, low, out):
    if pad(plan.rows[m]) > plan.rows[m]:
        out[...] = jnp.zeros_like(out)
    if plan.padded[m] > plan.cols[m]:
        none = jnp.zeros((plan.rows[m], plan.padded[m] - plan.cols[m]), jnp.bfloat16)
        high[:, plan.cols[m] :] = none
        low[:, plan.cols[m] :] = none


def load_rows(plan, m, rows, pair, grad, error, high, low, out):
    h, l = split(grad + error)
    high[rows, : plan.cols[m]] = h
    low[rows, : plan.cols[m]] = l
    out[:, rows] = three(pair, h, l, NT)


def blocks(count):
    return [pl.ds(r, min(LANES, count - r)) for r in range(0, count, LANES)]


def stream_kernel(plan, m, grad, error, warm, high, low, out, gbuf, ebuf, wbuf, sems, wsem):
    first = pltpu.make_async_copy(warm, wbuf, wsem.at[0])
    first.start()
    pieces = []
    for rows in blocks(plan.rows[m]):
        both = ((grad, gbuf), (error, ebuf))
        pieces.append((rows, [pltpu.make_async_copy(src.at[0, rows], buf.at[rows], sems.at[len(pieces), j]) for j, (src, buf) in enumerate(both)]))

    def start(i):
        for c in pieces[i][1] if i < len(pieces) else ():
            c.start()

    for i in range(DEPTH):
        start(i)
    blank(plan, m, high, low, out)
    first.wait()
    pair = stacked(wbuf[...])
    for i, (rows, copies) in enumerate(pieces):
        for c in copies:
            c.wait()
        start(i + DEPTH)
        load_rows(plan, m, rows, pair, gbuf[rows], ebuf[rows], high, low, out)


def hold_kernel(plan, m, grad, error, warm, high, low, out):
    blank(plan, m, high, low, out)
    pair = stacked(warm[...])
    for rows in blocks(plan.rows[m]):
        load_rows(plan, m, rows, pair, grad[0, rows], error[0, rows], high, low, out)


def load(plan, m, args, stream):
    half = jax.ShapeDtypeStruct((plan.rows[m], plan.padded[m]), jnp.bfloat16)
    full = pltpu.VMEM((plan.rows[m], plan.cols[m]), jnp.float32)
    outs = (half, half, f32(plan.rank, pad(plan.rows[m])))
    if not stream:
        return pl.pallas_call(
            functools.partial(hold_kernel, plan, m),
            out_shape=outs,
            in_specs=[VMEM] * 3,
            out_specs=(VMEM,) * 3,
            compiler_params=params(6),
            cost_estimate=cost(4),
            name="hold",
        )(*args)
    scratch = [full, full, pltpu.VMEM((plan.rank, plan.cols[m]), jnp.float32)]
    sems = [pltpu.SemaphoreType.DMA((len(blocks(plan.rows[m])), 2)), pltpu.SemaphoreType.DMA((1,))]
    return pl.pallas_call(
        functools.partial(stream_kernel, plan, m),
        out_shape=outs,
        in_specs=[ANY] * 3,
        out_specs=(VMEM,) * 3,
        scratch_shapes=scratch + sems,
        compiler_params=params(18),
        cost_estimate=cost(7),
        name="stream",
    )(*[pltpu.with_memory_space_constraint(a, pltpu.HBM) for a in args])


def right_slots(plan, m, odd, left, high, low, slots):
    pair = stacked(left[:, : plan.rows[m]])
    for j in range(plan.half):
        at = plan.columns(m, chunk_of(2 * j + odd))
        slots[j, :, plan.part_span(m)] = three(pair, high[:, at], low[:, at], NN)


def right_begin(m, scale, parts, inverse, left):
    term = parts[0][...] + parts[1][...]
    if scale is not None:
        term = dot32(inverse[m], term, NN) * scale
    left[...] = term
    return dot32(term, term, NT)


def gram_span(plan, m):
    return slice(plan.share + m * plan.rank, plan.share + (m + 1) * plan.rank)


def right_first_kernel(plan, m, scale, *refs):
    *inputs, odd, even, left = refs
    *parts_inverse, high, low = inputs
    gram = right_begin(m, scale, parts_inverse[:2], parts_inverse[-1], left)
    for parity, slots in enumerate((even, odd)):
        slots[:, :, plan.share :] = jnp.zeros((plan.half, plan.rank, LANES), jnp.float32)
        for j in range(plan.half):
            slots[j, :, gram_span(plan, m)] = gram
        right_slots(plan, m, parity, left, high, low, slots)


def right_odd_kernel(plan, m, scale, *refs):
    *inputs, odd, left, gram = refs
    *parts_inverse, _, high, low = inputs
    gram[...] = right_begin(m, scale, parts_inverse[:2], parts_inverse[-1], left)
    for j in range(plan.half):
        odd[j, :, gram_span(plan, m)] = gram[...]
    right_slots(plan, m, 1, left, high, low, odd)


def right_even_kernel(plan, m, left, gram, _, high, low, even):
    for j in range(plan.half):
        even[j, :, gram_span(plan, m)] = gram[...]
    right_slots(plan, m, 0, left, high, low, even)


def f32(*shape):
    return jax.ShapeDtypeStruct(shape, jnp.float32)


def right(plan, parts, matrix, inverse=None, scale=None):
    extra = [] if scale is None else [inverse]
    slots = f32(plan.half, plan.rank, plan.share + LANES)
    lefts = [f32(plan.rank, pad(r)) for r in plan.rows]

    def call(kernel, operands, outs, us, aliases={}):
        return pl.pallas_call(
            kernel,
            out_shape=outs,
            in_specs=[VMEM] * len(operands),
            out_specs=(VMEM,) * len(outs),
            input_output_aliases=aliases,
            compiler_params=params(5),
            cost_estimate=cost(us),
        )(*operands)

    first = functools.partial(right_first_kernel, plan, 1, scale)
    odd, even, left_1 = call(first, [*parts[1], *extra, *matrix[2:]], (slots, slots, lefts[1]), 1.8)
    second = functools.partial(right_odd_kernel, plan, 0, scale)
    operands = [*parts[0], *extra, odd, *matrix[:2]]
    odd, left_0, gram = call(second, operands, (slots, lefts[0], f32(plan.rank, plan.rank)), 1, {len(operands) - 3: 0})
    third = functools.partial(right_even_kernel, plan, 0)
    (even,) = call(third, [left_0, gram, even, *matrix[:2]], (slots,), 1, {2: 0})
    return odd, even, (left_0, left_1)


def left_kernel(plan, m, odd, *refs):
    *inputs, high, low, out = refs
    slots = inputs[0]
    if not odd and pad(plan.rows[m]) > plan.rows[m]:
        out[...] = jnp.zeros_like(out)
    if odd and pad(plan.rows[m]) > plan.rows[m]:
        out[:, plan.rows[m] :] = jnp.zeros((plan.rank, pad(plan.rows[m]) - plan.rows[m]), jnp.float32)
    terms = [(stacked(slots[j, :, plan.part_span(m)]), plan.columns(m, chunk_of(2 * j + odd))) for j in range(plan.half)]
    for r in range(0, plan.rows[m], 2 * LANES):
        rows = pl.ds(r, min(2 * LANES, plan.rows[m] - r))
        total = inputs[1][:, rows] if odd else None
        for pair, cols in terms:
            term = three(pair, high[rows, cols], low[rows, cols], NT)
            total = term if total is None else total + term
        out[:, rows] = total


def left(plan, near, far, matrix):
    def call(m, parity, *operands):
        return pl.pallas_call(
            functools.partial(left_kernel, plan, m, parity),
            out_shape=f32(plan.rank, pad(plan.rows[m])),
            in_specs=[VMEM] * (len(operands) + 2),
            out_specs=VMEM,
            compiler_params=params(5),
            cost_estimate=cost(1.2),
        )(*operands, *matrix[2 * m : 2 * m + 2])

    return [call(m, 1, far, call(m, 0, near)) for m in range(2)]


def factor_kernel(rank, gram, out):
    row = lax.broadcasted_iota(jnp.int32, (rank, 2 * rank), 0)
    col = lax.broadcasted_iota(jnp.int32, (rank, 2 * rank), 1)
    eye = jnp.where(row + rank == col, 1.0, 0.0)
    below = lax.broadcasted_iota(jnp.int32, (rank, 1), 0)
    work = []
    for m in range(2):
        sym = gram[:, m * rank : (m + 1) * rank]
        work.append(jnp.where(col < rank, jnp.concatenate([sym, sym], axis=1), eye))
    diag = [jnp.zeros((rank, 1), jnp.float32)] * 2
    for k in range(rank):
        for m in range(2):
            a = work[m]
            pivot = a[k : k + 1, k : k + 1]
            diag[m] = jnp.where(below == k, pivot, diag[m])
            ratio = jnp.where(below > k, a[:, k : k + 1], 0.0) / pivot
            work[m] = a - ratio * a[k : k + 1, :]
    for m in range(2):
        out[m] = work[m][:, rank:] / jnp.sqrt(diag[m])


def factor(plan, gram):
    return pl.pallas_call(
        functools.partial(factor_kernel, plan.rank),
        out_shape=jax.ShapeDtypeStruct((2, plan.rank, plan.rank), jnp.float32),
        in_specs=[VMEM],
        out_specs=VMEM,
        compiler_params=params(2),
        cost_estimate=cost(3),
        name="factor",
    )(gram)


def carry_slots(plan, scale, odd, slots, inverse, basis, matrix, q, stages, outs, sems):
    jobs = []
    for j in range(plan.half):
        chunk = chunk_of(2 * j + odd)
        for m, (h, l) in enumerate((matrix[:2], matrix[2:])):
            span = plan.part_span(m)
            q[j, :, span] = dot32(inverse[m], slots[j, :, span], NN) * scale
            high, low = split(q[j, :, span])
            triple = jnp.concatenate([high, low, high], axis=0)
            at = plan.columns(m, chunk)
            for r in range(0, plan.rows[m], 2 * LANES):
                rows = pl.ds(r, min(2 * LANES, plan.rows[m] - r))
                b = basis[pl.ds(plan.row_at[m] + r, rows.size)]
                whole = h[rows, at].astype(jnp.float32) + l[rows, at].astype(jnp.float32)
                stages[m][j, rows] = whole - dot(b, triple, NN)
            last = plan.cols[m] - (plan.shards - 1) * plan.part[m]

            def copy(m=m, j=j, at=at, n=plan.part[m]):
                at = at if n == plan.part[m] else pl.ds(plan.cols[m] - n, n)
                return pltpu.make_async_copy(stages[m].at[j, :, pl.ds(0, n)], outs[m].at[0, :, at], sems.at[m, j])

            def each(act, copy=copy, chunk=chunk, last=last, full=last == plan.part[m]):
                if full:
                    act(copy())
                else:
                    pl.when(chunk < plan.shards - 1)(lambda: act(copy()))
                    pl.when(chunk == plan.shards - 1)(lambda: act(copy(n=last)))

            each(lambda c: c.start())
            jobs.append(each)
    for each in jobs:
        each(lambda c: c.wait())


def basis_kernel(plan, inverse, left_0, left_1, basis):
    for m in range(2):
        high, low = split(dot32(inverse[m], (left_0, left_1)[m][...], NN))
        high, low = high.astype(jnp.float32), low.astype(jnp.float32)
        basis[plan.row_span(m)] = jnp.concatenate([high, high, low], axis=0).T.astype(jnp.bfloat16)


def basis_of(plan, inverse, left):
    return pl.pallas_call(
        functools.partial(basis_kernel, plan),
        out_shape=jax.ShapeDtypeStruct((plan.row_all, 3 * plan.rank), jnp.bfloat16),
        in_specs=[VMEM] * 3,
        out_specs=VMEM,
        compiler_params=params(4),
        cost_estimate=cost(0.8),
        name="basis",
    )(inverse, *left)


def carry_first_kernel(plan, scale, slots, inverse, basis, ha, la, hf, lf, ca, cf, q, sa, sf, sems):
    carry_slots(plan, scale, 0, slots, inverse, basis, (ha, la, hf, lf), q, (sa, sf), (ca, cf), sems)


def carry_second_kernel(plan, scale, slots, inverse, basis, other, ia, jf, ha, la, hf, lf, ca, cf, qa, qf, q, sa, sf, sems):
    carry_slots(plan, scale, 1, slots, inverse, basis, (ha, la, hf, lf), q, (sa, sf), (ca, cf), sems)
    place = lax.axis_index("shard")
    for c in range(plan.shards):
        slot = lax.bitwise_xor(jnp.int32(c), place)
        row = slot >> 1
        for m, out in enumerate((qa, qf)):
            start = c * plan.part[m]
            n = min(plan.part[m], plan.cols[m] - start)
            span = slice(plan.part_at[m], plan.part_at[m] + n)
            out[:, start : start + n] = jnp.where((slot & 1) == 0, other[row, :, span], q[row, :, span])


def carry(plan, even, odd, inverse, basis, matrix, scale):
    half, rank, rows, cols = plan.half, plan.rank, plan.rows, plan.cols
    stage = [pltpu.VMEM((half, rows[m], plan.part[m]), jnp.float32) for m in range(2)] + [pltpu.SemaphoreType.DMA((2, half))]
    outs = tuple(f32(1, rows[m], cols[m]) for m in range(2))
    ca, cf, q = pl.pallas_call(
        functools.partial(carry_first_kernel, plan, scale),
        out_shape=outs + (f32(half, rank, plan.share),),
        in_specs=[VMEM] * 7,
        out_specs=(ANY, ANY, VMEM),
        scratch_shapes=stage,
        compiler_params=params(16),
        cost_estimate=cost(4),
        name="carry_first",
    )(even, inverse, basis, *matrix)
    return pl.pallas_call(
        functools.partial(carry_second_kernel, plan, scale),
        out_shape=outs + tuple(f32(rank, cols[m]) for m in range(2)),
        in_specs=[VMEM] * 4 + [ANY] * 2 + [VMEM] * 4,
        out_specs=(ANY, ANY, VMEM, VMEM),
        scratch_shapes=[pltpu.VMEM((half, rank, plan.share), jnp.float32)] + stage,
        input_output_aliases={4: 0, 5: 1},
        compiler_params=params(16),
        cost_estimate=cost(4),
        name="carry_second",
    )(odd, inverse, basis, q, ca, cf, *matrix)


def swapped(x, axis, offset):
    return lax.ppermute(x, axis, [(i, i ^ offset) for i in range(lax.axis_size(axis))])


def exchanged(x, axis):
    return [x] + [swapped(x, axis, k) for k in range(1, lax.axis_size(axis))]


def offsets(size):
    found = [size - 1]
    while found[-1] > 1:
        found.append(found[-1] // 2)
    return found


def paired(terms, axis):
    hops = offsets(lax.axis_size(axis))
    parts = []
    for m, x in enumerate(terms):
        order = hops if m else hops[::-1]
        for step, offset in enumerate(order):
            y = swapped(x, axis, offset)
            if step + 1 < len(order):
                x = x + y
        parts.append((x, y))
    return parts


def gathered(odd, even):
    mine = even + swapped(odd, "shard", 1)
    return tree([mine[0]] + [swapped(mine[j], "shard", 2 * j) for j in range(1, mine.shape[0])])


def spread(share, half):
    return jnp.stack([share] + [swapped(share, "shard", 2 * j) for j in range(1, half)])


def compress(ag, ae, wa, fg, fe, wf):
    plan = Plan((ag.shape[1], fg.shape[1]), (ag.shape[2], fg.shape[2]), wa.shape[0], lax.axis_size("shard"))
    scale = 1.0 / lax.axis_size("dp")
    *second, left_1 = load(plan, 1, (fg, fe, wf), True)
    *first, left_0 = load(plan, 0, (ag, ae, wa), False)
    matrix = first + second
    terms = [left_0, left_1]
    inverse = None
    for sweep in range(ITERS):
        parts = paired(terms, "dp")
        odd, even, whole = right(plan, parts, matrix, inverse, None if inverse is None else scale)
        joint = gathered(odd, even)
        inverse = factor(plan, joint[:, plan.share :])
        share = tree(exchanged(joint[:, : plan.share], "dp"))
        if sweep + 1 == ITERS:
            basis = basis_of(plan, inverse, whole)
            share, inverse, basis = lax.optimization_barrier((share, inverse, basis))
        else:
            share, inverse = lax.optimization_barrier((share, inverse))
        near = spread(share, plan.half)
        far = swapped(near, "shard", 1)
        if sweep + 1 < ITERS:
            terms = left(plan, near, far, matrix)
    return carry(plan, near, far, inverse, basis, matrix, scale)


def solution(mesh):
    tall = P("dp", "shard", None)
    return jax.shard_map(
        compress,
        mesh=mesh,
        in_specs=(tall, tall, P(), tall, tall, P()),
        out_specs=(tall, tall, P(), P()),
        check_vma=False,
    )
```

time: 504 us -> 127 us (0.25); the launches traced: 495 us -> 127 us
  waiting for transfers between devices: 188 us -> 46.2 us
  blocking collectives: 126 us -> 0 us
  matrix products: 112 us -> 0 us
  other arithmetic: 46.2 us -> 0.33 us
  Pallas kernels: 0 us -> 40.1 us
  starting transfers between devices: 0.33 us -> 38.8 us
  between operations: 14.8 us -> 1.02 us
  local copies, waits for them, and re-layouts: 8.22 us -> 0.08 us
    psum x4 -> x0, waiting for transfers between devices: 104 us -> none  [the longest x3 66.5 us: shards(): lax.psum((left_product(first_matrix, first_factor), left_product(second_m...]
    psum x4 -> x0, blocking collectives: 86.9 us -> none  [the longest x2 45 us: shards(): lax.psum((right_product(first_left, first_left), right_product(second_lef...]
    dot_general x12 -> x0, matrix products: 77.8 us -> none  [the longest x4 36.7 us: left_product(): lax.dot_general(matrix, factor, (((1,), (1,)), ((), ())), precision=highe...]
    unnamed x10 -> x0, waiting for transfers between devices: 48 us -> none
    ppermute x0 -> x30, waiting for transfers between devices: none -> 46.2 us  [swapped(): lax.ppermute(x, axis, [(i, i ^ offset) for i in range(lax.axis_size(axis))])]
    pallas_call x0 -> x17, Pallas kernels: none -> 40.1 us  [the longest x1 9.03 us: load(): pl.pallas_call(functools.partial(stream_kernel, plan, m), out_shape=outs,...]
    ppermute x0 -> x30, starting transfers between devices: none -> 38.8 us  [swapped(): lax.ppermute(x, axis, [(i, i ^ offset) for i in range(lax.axis_size(axis))])]
    all_gather x4 -> x0, blocking collectives: 38.8 us -> none  [the longest x2 20.1 us: shards(): lax.all_gather(first_share / replicas, 'shard', axis=1, tiled=True)]
  transfers between devices with their start and end apart: 8 -> 30, of which waited for: 6 -> 23; matrix products, arithmetic and copies ran while one was open for 12% -> 0% of each run, Pallas kernels for 0% -> 18%
where the time goes in v1:
time: 127 us
  waiting for transfers between devices  46.2 us (36%)
  Pallas kernels  40.1 us (32%)
  starting transfers between devices  38.8 us (31%)
    ppermute x30, waiting for transfers between devices, swapped(): lax.ppermute(x, axis, [(i, i ^ offset) for i in range(lax.axis_size(axis))])  46.2 us
    ppermute x30, starting transfers between devices, swapped(): lax.ppermute(x, axis, [(i, i ^ offset) for i in range(lax.axis_size(axis))])  38.8 us
    pallas_call x1, Pallas kernels, load(): pl.pallas_call(functools.partial(stream_kernel, plan, m), out_shape=outs,...  9.03 us
    pallas_call x6, Pallas kernels, call(): pl.pallas_call(kernel, out_shape=outs, in_specs=[VMEM] * len(operands), o...  7.29 us
    pallas_call x2, Pallas kernels, factor(): pl.pallas_call(functools.partial(factor_kernel, plan.rank), out_shape=jax...  5.86 us
    pallas_call x4, Pallas kernels, call(): pl.pallas_call(functools.partial(left_kernel, plan, m, parity), out_shape...  5.24 us
    pallas_call x1, Pallas kernels, carry(): pl.pallas_call(functools.partial(carry_second_kernel, plan, scale), out_s...  5.04 us
    pallas_call x1, Pallas kernels, carry(): pl.pallas_call(functools.partial(carry_first_kernel, plan, scale), out_sh...  4.17 us
  transfers between devices with their start and end apart: 30, of which 23 were waited for; matrix products, arithmetic and copies ran while one was open for 0% of the time, Pallas kernels for 18%

profile of v1, /device:TPU:0, one launch (start us, length us, event | category | flops | bytes accessed | tf_op | source)
XLA Modules:
  0.0 126.6 jit_solution(11300293578116477610)
XLA Ops:
  0.7 9.0 %stream.1 = (bf16[992,2048]{1,0:T(8,128)(2,1)S(1)}, bf16[992,2048]{1,0:T(8,128)(2,1)S(1)}, f32[32,1024]{1,0:T(8,128)S(1)}) custom-call(f32[1,992,2048]{2,1,0:T(8,128)} %grad.3, f32[1,992,2048]{2,1,0:T(8,128)} %error.3, f32[32,2048]{1,0:T(8,128)} %warm.3), custom_call_target="tpu_custom_call" | custom-call | bytes 21000000 | tf_op jit(solution)/shard_map/stream/pallas_call | solution.py:160
  9.7 5.1 %collective-permute-start.2 = (f32[32,1024]{1,0:T(8,128)S(1)}, f32[32,1024]{1,0:T(8,128)S(1)}, u32[]{:S(2)}, u32[]{:S(2)}) collective-permute-start(f32[32,1024]{1,0:T(8,128)S(1)} %get-tuple-element.30), channel_id=1, source_target_pairs={{0,24},{8,16},{16,8},{24,0},{1,25},{9,17},{17,9},{25,1},{2,26},{10... | collective-permute-start | bytes 393224 | tf_op jit(solution)/shard_map/ppermute | solution.py:409
  14.9 3.0 %hold.1 = (bf16[496,4096]{1,0:T(8,128)(2,1)S(1)}, bf16[496,4096]{1,0:T(8,128)(2,1)S(1)}, f32[32,512]{1,0:T(8,128)S(1)}) custom-call(f32[1,496,3968]{2,1,0:T(8,128)S(1)} %copy-done, f32[1,496,3968]{2,1,0:T(8,128)S(1)} %copy-done.1, f32[32,3968]{1,0:T(8,128)S(1)} %copy-done.2), custom_call_target="tpu_custom_call" | custom-call | bytes 12000000 | tf_op jit(solution)/shard_map/hold/pallas_call | solution.py:149
  18.5 2.5 %collective-permute-start.3 = (f32[32,1024]{1,0:T(8,128)S(1)}, f32[32,1024]{1,0:T(8,128)S(1)}, u32[]{:S(2)}, u32[]{:S(2)}) collective-permute-start(f32[32,1024]{1,0:T(8,128)S(1)} %add.55.refs_0_), channel_id=1, source_target_pairs={{0,8},{8,0},{16,24},{24,16},{1,9},{9,1},{17,25},{25,17},{2,10},{10... | collective-permute-start | bytes 393224 | tf_op jit(solution)/shard_map/ppermute | solution.py:409
  21.0 4.2 %collective-permute-done = f32[32,512]{1,0:T(8,128)S(1)} collective-permute-done((f32[32,512]{1,0:T(8,128)S(1)}, f32[32,512]{1,0:T(8,128)S(1)}, u32[]{:S(2)}, u32[]{:S(2)}) %collective-permute-start) | collective-permute-done | bytes 65568 | tf_op jit(solution)/shard_map/ppermute | solution.py:409
  25.3 2.7 %collective-permute-start.1 = (f32[32,512]{1,0:T(8,128)S(1)}, f32[32,512]{1,0:T(8,128)S(1)}, u32[]{:S(2)}, u32[]{:S(2)}) collective-permute-start(f32[32,512]{1,0:T(8,128)S(1)} %add.54.refs_0_), channel_id=1, source_target_pairs={{0,24},{8,16},{16,8},{24,0},{1,25},{9,17},{17,9},{25,1},{2,26},{10... | collective-permute-start | bytes 196616 | tf_op jit(solution)/shard_map/ppermute | solution.py:409
  34.2 2.5 %collective-permute-start.7 = (f32[32,896]{1,0:T(8,128)S(1)}, f32[32,896]{1,0:T(8,128)S(1)}, u32[]{:S(2)}, u32[]{:S(2)}) collective-permute-start(f32[32,896]{1,0:T(8,128)S(1)} %get-tuple-element.57), channel_id=1, source_target_pairs={{0,6},{1,7},{2,4},{3,5},{4,2},{5,3},{6,0},{7,1},{8,14},{9,15},{10,... | collective-permute-start | bytes 344072 | tf_op jit(solution)/shard_map/ppermute | solution.py:409
  37.7 3.4 %collective-permute-done.7 = f32[32,896]{1,0:T(8,128)S(1)} collective-permute-done((f32[32,896]{1,0:T(8,128)S(1)}, f32[32,896]{1,0:T(8,128)S(1)}, u32[]{:S(2)}, u32[]{:S(2)}) %collective-permute-start.7) | collective-permute-done | bytes 114720 | tf_op jit(solution)/shard_map/ppermute | solution.py:409
  43.0 2.6 %collective-permute-start.10 = (f32[32,768]{1,0:T(8,128)S(1)}, f32[32,768]{1,0:T(8,128)S(1)}, u32[]{:S(2)}, u32[]{:S(2)}) collective-permute-start(f32[32,768]{1,0:T(8,128)S(1)} %slice.52), channel_id=1, source_target_pairs={{0,24},{8,16},{16,8},{24,0},{1,25},{9,17},{17,9},{25,1},{2,26},{10... | collective-permute-start | bytes 294920 | tf_op jit(solution)/shard_map/ppermute | solution.py:409
  46.5 2.9 %factor.2.refs_2_ = f32[2,32,32]{2,1,0:T(8,128)S(1)} custom-call(f32[32,128]{1,0:T(8,128)S(1)} %slice.53.gram), custom_call_target="tpu_custom_call" | custom-call | bytes 9000000 | tf_op jit(solution)/shard_map/factor/pallas_call | solution.py:300
  51.1 3.6 %collective-permute-done.8 = f32[32,768]{1,0:T(8,128)S(1)} collective-permute-done((f32[32,768]{1,0:T(8,128)S(1)}, f32[32,768]{1,0:T(8,128)S(1)}, u32[]{:S(2)}, u32[]{:S(2)}) %collective-permute-start.8) | collective-permute-done | bytes 98336 | tf_op jit(solution)/shard_map/ppermute | solution.py:409
  54.7 3.0 %collective-permute-start.13 = (f32[32,768]{1,0:T(8,128)S(1)}, f32[32,768]{1,0:T(8,128)S(1)}, u32[]{:S(2)}, u32[]{:S(2)}) collective-permute-start(f32[32,768]{1,0:T(8,128)S(1)} %add_add_fusion.1), channel_id=1, source_target_pairs={{0,6},{1,7},{2,4},{3,5},{4,2},{5,3},{6,0},{7,1},{8,14},{9,15},{10,... | collective-permute-start | bytes 294920 | tf_op jit(solution)/shard_map/ppermute | solution.py:409
  58.4 2.1 %collective-permute-done.13 = f32[32,768]{1,0:T(8,128)S(1)} collective-permute-done((f32[32,768]{1,0:T(8,128)S(1)}, f32[32,768]{1,0:T(8,128)S(1)}, u32[]{:S(2)}, u32[]{:S(2)}) %collective-permute-start.13) | collective-permute-done | bytes 98336 | tf_op jit(solution)/shard_map/ppermute | solution.py:409
  65.9 2.4 %collective-permute-start.17 = (f32[32,1024]{1,0:T(8,128)S(1)}, f32[32,1024]{1,0:T(8,128)S(1)}, u32[]{:S(2)}, u32[]{:S(2)}) collective-permute-start(f32[32,1024]{1,0:T(8,128)S(1)} %shard_map.99), channel_id=1, source_target_pairs={{0,24},{8,16},{16,8},{24,0},{1,25},{9,17},{17,9},{25,1},{2,26},{10... | collective-permute-start | bytes 393224 | tf_op jit(solution)/shard_map/ppermute | solution.py:409
  70.8 2.5 %collective-permute-done.17 = f32[32,1024]{1,0:T(8,128)S(1)} collective-permute-done((f32[32,1024]{1,0:T(8,128)S(1)}, f32[32,1024]{1,0:T(8,128)S(1)}, u32[]{:S(2)}, u32[]{:S(2)}) %collective-permute-start.17) | collective-permute-done | bytes 131104 | tf_op jit(solution)/shard_map/ppermute | solution.py:409
  75.4 4.1 %collective-permute-done.15 = f32[32,512]{1,0:T(8,128)S(1)} collective-permute-done((f32[32,512]{1,0:T(8,128)S(1)}, f32[32,512]{1,0:T(8,128)S(1)}, u32[]{:S(2)}, u32[]{:S(2)}) %collective-permute-start.15) | collective-permute-done | bytes 65568 | tf_op jit(solution)/shard_map/ppermute | solution.py:409
  79.5 2.4 %collective-permute-start.16 = (f32[32,512]{1,0:T(8,128)S(1)}, f32[32,512]{1,0:T(8,128)S(1)}, u32[]{:S(2)}, u32[]{:S(2)}) collective-permute-start(f32[32,512]{1,0:T(8,128)S(1)} %add.63.refs_0_), channel_id=1, source_target_pairs={{0,24},{8,16},{16,8},{24,0},{1,25},{9,17},{17,9},{25,1},{2,26},{10... | collective-permute-start | bytes 196616 | tf_op jit(solution)/shard_map/ppermute | solution.py:409
  92.1 3.4 %collective-permute-done.22 = f32[32,896]{1,0:T(8,128)S(1)} collective-permute-done((f32[32,896]{1,0:T(8,128)S(1)}, f32[32,896]{1,0:T(8,128)S(1)}, u32[]{:S(2)}, u32[]{:S(2)}) %collective-permute-start.22) | collective-permute-done | bytes 114720 | tf_op jit(solution)/shard_map/ppermute | solution.py:409
  97.6 2.5 %collective-permute-start.25 = (f32[32,768]{1,0:T(8,128)S(1)}, f32[32,768]{1,0:T(8,128)S(1)}, u32[]{:S(2)}, u32[]{:S(2)}) collective-permute-start(f32[32,768]{1,0:T(8,128)S(1)} %slice.58), channel_id=1, source_target_pairs={{0,24},{8,16},{16,8},{24,0},{1,25},{9,17},{17,9},{25,1},{2,26},{10... | collective-permute-start | bytes 294920 | tf_op jit(solution)/shard_map/ppermute | solution.py:409
  101.1 2.9 %factor.3.inverse = f32[2,32,32]{2,1,0:T(8,128)S(1)} custom-call(f32[32,128]{1,0:T(8,128)S(1)} %slice.59.gram), custom_call_target="tpu_custom_call" | custom-call | bytes 9000000 | tf_op jit(solution)/shard_map/factor/pallas_call | solution.py:300
  105.6 3.7 %collective-permute-done.23 = f32[32,768]{1,0:T(8,128)S(1)} collective-permute-done((f32[32,768]{1,0:T(8,128)S(1)}, f32[32,768]{1,0:T(8,128)S(1)}, u32[]{:S(2)}, u32[]{:S(2)}) %collective-permute-start.23) | collective-permute-done | bytes 98336 | tf_op jit(solution)/shard_map/ppermute | solution.py:409
  112.9 2.8 %collective-permute-done.28 = f32[32,768]{1,0:T(8,128)S(1)} collective-permute-done((f32[32,768]{1,0:T(8,128)S(1)}, f32[32,768]{1,0:T(8,128)S(1)}, u32[]{:S(2)}, u32[]{:S(2)}) %collective-permute-start.28) | collective-permute-done | bytes 98336 | tf_op jit(solution)/shard_map/ppermute | solution.py:409
  117.2 4.2 %carry_first.1 = (f32[1,496,3968]{2,1,0:T(8,128)}, f32[1,992,2048]{2,1,0:T(8,128)}, f32[4,32,768]{2,1,0:T(8,128)S(1)}) custom-call(f32[4,32,768]{2,1,0:T(8,128)S(1)} %pad_maximum_fusion.1.slots, f32[2,32,32]{2,1,0:T(8,128)S(1)} %factor.3.inverse, bf16[1536,96]{1,0:T(8,128)(2,1)S(1)} %basis.1, ...), custom_call_target="tpu_custom_call" | custom-call | bytes 12000000 | tf_op jit(solution)/shard_map/carry_first/pallas_call | solution.py:385
  121.4 5.0 %carry_second.1 = (f32[1,496,3968]{2,1,0:T(8,128)}, f32[1,992,2048]{2,1,0:T(8,128)}, f32[32,3968]{1,0:T(8,128)}, f32[32,2048]{1,0:T(8,128)}) custom-call(f32[4,32,768]{2,1,0:T(8,128)S(1)} %collective-permute-done.29.slots, f32[2,32,32]{2,1,0:T(8,128)S(1)} %factor.3.inverse, ...), custom_call_target="tpu_custom_call", output_to_operand_aliasing={{0}: (4, {}), {1}: (5, {})} | custom-call | bytes 12000000 | tf_op jit(solution)/shard_map/carry_second/pallas_call | solution.py:395
  (77 shorter events, 42.9 us)
Async XLA Ops:
  9.7 8.7 %collective-permute-start.2 = (f32[32,1024]{1,0:T(8,128)S(1)}, f32[32,1024]{1,0:T(8,128)S(1)}, u32[]{:S(2)}, u32[]{:S(2)}) collective-permute-start(f32[32,1024]{1,0:T(8,128)S(1)} %get-tuple-element.30), channel_id=1, source_target_pairs={{0,24},{8,16},{16,8},{24,0},{1,25},{9,17},{17,9},{25,1},{2,26},{10... | collective-permute-start | bytes 393224 | tf_op jit(solution)/shard_map/ppermute | solution.py:409
  18.5 9.5 %collective-permute-start.3 = (f32[32,1024]{1,0:T(8,128)S(1)}, f32[32,1024]{1,0:T(8,128)S(1)}, u32[]{:S(2)}, u32[]{:S(2)}) collective-permute-start(f32[32,1024]{1,0:T(8,128)S(1)} %add.55.refs_0_), channel_id=1, source_target_pairs={{0,8},{8,0},{16,24},{24,16},{1,9},{9,1},{17,25},{25,17},{2,10},{10... | collective-permute-start | bytes 393224 | tf_op jit(solution)/shard_map/ppermute | solution.py:409
  25.3 6.2 %collective-permute-start.1 = (f32[32,512]{1,0:T(8,128)S(1)}, f32[32,512]{1,0:T(8,128)S(1)}, u32[]{:S(2)}, u32[]{:S(2)}) collective-permute-start(f32[32,512]{1,0:T(8,128)S(1)} %add.54.refs_0_), channel_id=1, source_target_pairs={{0,24},{8,16},{16,8},{24,0},{1,25},{9,17},{17,9},{25,1},{2,26},{10... | collective-permute-start | bytes 196616 | tf_op jit(solution)/shard_map/ppermute | solution.py:409
  34.2 7.0 %collective-permute-start.7 = (f32[32,896]{1,0:T(8,128)S(1)}, f32[32,896]{1,0:T(8,128)S(1)}, u32[]{:S(2)}, u32[]{:S(2)}) collective-permute-start(f32[32,896]{1,0:T(8,128)S(1)} %get-tuple-element.57), channel_id=1, source_target_pairs={{0,6},{1,7},{2,4},{3,5},{4,2},{5,3},{6,0},{7,1},{8,14},{9,15},{10,... | collective-permute-start | bytes 344072 | tf_op jit(solution)/shard_map/ppermute | solution.py:409
  36.7 6.2 %collective-permute-start.6 = (f32[32,896]{1,0:T(8,128)S(1)}, f32[32,896]{1,0:T(8,128)S(1)}, u32[]{:S(2)}, u32[]{:S(2)}) collective-permute-start(f32[32,896]{1,0:T(8,128)S(1)} %get-tuple-element.58), channel_id=1, source_target_pairs={{0,2},{1,3},{2,0},{3,1},{4,6},{5,7},{6,4},{7,5},{8,10},{9,11},{10,... | collective-permute-start | bytes 344072 | tf_op jit(solution)/shard_map/ppermute | solution.py:409
  37.2 5.6 %collective-permute-start.5 = (f32[32,896]{1,0:T(8,128)S(1)}, f32[32,896]{1,0:T(8,128)S(1)}, u32[]{:S(2)}, u32[]{:S(2)}) collective-permute-start(f32[32,896]{1,0:T(8,128)S(1)} %get-tuple-element.59), channel_id=1, source_target_pairs={{0,4},{1,5},{2,6},{3,7},{4,0},{5,1},{6,2},{7,3},{8,12},{9,13},{10,... | collective-permute-start | bytes 344072 | tf_op jit(solution)/shard_map/ppermute | solution.py:409
  42.9 6.5 %collective-permute-start.9 = (f32[32,768]{1,0:T(8,128)S(1)}, f32[32,768]{1,0:T(8,128)S(1)}, u32[]{:S(2)}, u32[]{:S(2)}) collective-permute-start(f32[32,768]{1,0:T(8,128)S(1)} %slice.52), channel_id=1, source_target_pairs={{0,8},{8,0},{16,24},{24,16},{1,9},{9,1},{17,25},{25,17},{2,10},{10... | collective-permute-start | bytes 294920 | tf_op jit(solution)/shard_map/ppermute | solution.py:409
  43.0 8.1 %collective-permute-start.10 = (f32[32,768]{1,0:T(8,128)S(1)}, f32[32,768]{1,0:T(8,128)S(1)}, u32[]{:S(2)}, u32[]{:S(2)}) collective-permute-start(f32[32,768]{1,0:T(8,128)S(1)} %slice.52), channel_id=1, source_target_pairs={{0,24},{8,16},{16,8},{24,0},{1,25},{9,17},{17,9},{25,1},{2,26},{10... | collective-permute-start | bytes 294920 | tf_op jit(solution)/shard_map/ppermute | solution.py:409
  45.6 9.1 %collective-permute-start.8 = (f32[32,768]{1,0:T(8,128)S(1)}, f32[32,768]{1,0:T(8,128)S(1)}, u32[]{:S(2)}, u32[]{:S(2)}) collective-permute-start(f32[32,768]{1,0:T(8,128)S(1)} %slice.52), channel_id=1, source_target_pairs={{0,16},{8,24},{16,0},{24,8},{1,17},{9,25},{17,1},{25,9},{2,18},{10... | collective-permute-start | bytes 294920 | tf_op jit(solution)/shard_map/ppermute | solution.py:409
  54.7 5.8 %collective-permute-start.13 = (f32[32,768]{1,0:T(8,128)S(1)}, f32[32,768]{1,0:T(8,128)S(1)}, u32[]{:S(2)}, u32[]{:S(2)}) collective-permute-start(f32[32,768]{1,0:T(8,128)S(1)} %add_add_fusion.1), channel_id=1, source_target_pairs={{0,6},{1,7},{2,4},{3,5},{4,2},{5,3},{6,0},{7,1},{8,14},{9,15},{10,... | collective-permute-start | bytes 294920 | tf_op jit(solution)/shard_map/ppermute | solution.py:409
  57.7 4.9 %collective-permute-start.11 = (f32[32,768]{1,0:T(8,128)S(1)}, f32[32,768]{1,0:T(8,128)S(1)}, u32[]{:S(2)}, u32[]{:S(2)}) collective-permute-start(f32[32,768]{1,0:T(8,128)S(1)} %add_add_fusion.1), channel_id=1, source_target_pairs={{0,2},{1,3},{2,0},{3,1},{4,6},{5,7},{6,4},{7,5},{8,10},{9,11},{10,... | collective-permute-start | bytes 294920 | tf_op jit(solution)/shard_map/ppermute | solution.py:409
  65.9 7.4 %collective-permute-start.17 = (f32[32,1024]{1,0:T(8,128)S(1)}, f32[32,1024]{1,0:T(8,128)S(1)}, u32[]{:S(2)}, u32[]{:S(2)}) collective-permute-start(f32[32,1024]{1,0:T(8,128)S(1)} %shard_map.99), channel_id=1, source_target_pairs={{0,24},{8,16},{16,8},{24,0},{1,25},{9,17},{17,9},{25,1},{2,26},{10... | collective-permute-start | bytes 393224 | tf_op jit(solution)/shard_map/ppermute | solution.py:409
  73.3 8.6 %collective-permute-start.18 = (f32[32,1024]{1,0:T(8,128)S(1)}, f32[32,1024]{1,0:T(8,128)S(1)}, u32[]{:S(2)}, u32[]{:S(2)}) collective-permute-start(f32[32,1024]{1,0:T(8,128)S(1)} %add.64.refs_0_), channel_id=1, source_target_pairs={{0,8},{8,0},{16,24},{24,16},{1,9},{9,1},{17,25},{25,17},{2,10},{10... | collective-permute-start | bytes 393224 | tf_op jit(solution)/shard_map/ppermute | solution.py:409
  73.4 6.1 %collective-permute-start.15 = (f32[32,512]{1,0:T(8,128)S(1)}, f32[32,512]{1,0:T(8,128)S(1)}, u32[]{:S(2)}, u32[]{:S(2)}) collective-permute-start(f32[32,512]{1,0:T(8,128)S(1)} %shard_map.97), channel_id=1, source_target_pairs={{0,8},{8,0},{16,24},{24,16},{1,9},{9,1},{17,25},{25,17},{2,10},{10... | collective-permute-start | bytes 196616 | tf_op jit(solution)/shard_map/ppermute | solution.py:409
  79.5 6.1 %collective-permute-start.16 = (f32[32,512]{1,0:T(8,128)S(1)}, f32[32,512]{1,0:T(8,128)S(1)}, u32[]{:S(2)}, u32[]{:S(2)}) collective-permute-start(f32[32,512]{1,0:T(8,128)S(1)} %add.63.refs_0_), channel_id=1, source_target_pairs={{0,24},{8,16},{16,8},{24,0},{1,25},{9,17},{17,9},{25,1},{2,26},{10... | collective-permute-start | bytes 196616 | tf_op jit(solution)/shard_map/ppermute | solution.py:409
  88.6 7.0 %collective-permute-start.22 = (f32[32,896]{1,0:T(8,128)S(1)}, f32[32,896]{1,0:T(8,128)S(1)}, u32[]{:S(2)}, u32[]{:S(2)}) collective-permute-start(f32[32,896]{1,0:T(8,128)S(1)} %get-tuple-element.54), channel_id=1, source_target_pairs={{0,6},{1,7},{2,4},{3,5},{4,2},{5,3},{6,0},{7,1},{8,14},{9,15},{10,... | collective-permute-start | bytes 344072 | tf_op jit(solution)/shard_map/ppermute | solution.py:409
  90.4 7.1 %collective-permute-start.21 = (f32[32,896]{1,0:T(8,128)S(1)}, f32[32,896]{1,0:T(8,128)S(1)}, u32[]{:S(2)}, u32[]{:S(2)}) collective-permute-start(f32[32,896]{1,0:T(8,128)S(1)} %get-tuple-element.55), channel_id=1, source_target_pairs={{0,2},{1,3},{2,0},{3,1},{4,6},{5,7},{6,4},{7,5},{8,10},{9,11},{10,... | collective-permute-start | bytes 344072 | tf_op jit(solution)/shard_map/ppermute | solution.py:409
  91.9 5.6 %collective-permute-start.20 = (f32[32,896]{1,0:T(8,128)S(1)}, f32[32,896]{1,0:T(8,128)S(1)}, u32[]{:S(2)}, u32[]{:S(2)}) collective-permute-start(f32[32,896]{1,0:T(8,128)S(1)} %get-tuple-element.56), channel_id=1, source_target_pairs={{0,4},{1,5},{2,6},{3,7},{4,0},{5,1},{6,2},{7,3},{8,12},{9,13},{10,... | collective-permute-start | bytes 344072 | tf_op jit(solution)/shard_map/ppermute | solution.py:409
  97.5 6.9 %collective-permute-start.24 = (f32[32,768]{1,0:T(8,128)S(1)}, f32[32,768]{1,0:T(8,128)S(1)}, u32[]{:S(2)}, u32[]{:S(2)}) collective-permute-start(f32[32,768]{1,0:T(8,128)S(1)} %slice.58), channel_id=1, source_target_pairs={{0,8},{8,0},{16,24},{24,16},{1,9},{9,1},{17,25},{25,17},{2,10},{10... | collective-permute-start | bytes 294920 | tf_op jit(solution)/shard_map/ppermute | solution.py:409
  97.6 8.0 %collective-permute-start.25 = (f32[32,768]{1,0:T(8,128)S(1)}, f32[32,768]{1,0:T(8,128)S(1)}, u32[]{:S(2)}, u32[]{:S(2)}) collective-permute-start(f32[32,768]{1,0:T(8,128)S(1)} %slice.58), channel_id=1, source_target_pairs={{0,24},{8,16},{16,8},{24,0},{1,25},{9,17},{17,9},{25,1},{2,26},{10... | collective-permute-start | bytes 294920 | tf_op jit(solution)/shard_map/ppermute | solution.py:409
  100.1 9.1 %collective-permute-start.23 = (f32[32,768]{1,0:T(8,128)S(1)}, f32[32,768]{1,0:T(8,128)S(1)}, u32[]{:S(2)}, u32[]{:S(2)}) collective-permute-start(f32[32,768]{1,0:T(8,128)S(1)} %slice.58), channel_id=1, source_target_pairs={{0,16},{8,24},{16,0},{24,8},{1,17},{9,25},{17,1},{25,9},{2,18},{10... | collective-permute-start | bytes 294920 | tf_op jit(solution)/shard_map/ppermute | solution.py:409
  109.3 6.4 %collective-permute-start.28 = (f32[32,768]{1,0:T(8,128)S(1)}, f32[32,768]{1,0:T(8,128)S(1)}, u32[]{:S(2)}, u32[]{:S(2)}) collective-permute-start(f32[32,768]{1,0:T(8,128)S(1)} %add_add_fusion), channel_id=1, source_target_pairs={{0,6},{1,7},{2,4},{3,5},{4,2},{5,3},{6,0},{7,1},{8,14},{9,15},{10,... | collective-permute-start | bytes 294920 | tf_op jit(solution)/shard_map/ppermute | solution.py:409
  111.1 5.1 %collective-permute-start.27 = (f32[32,768]{1,0:T(8,128)S(1)}, f32[32,768]{1,0:T(8,128)S(1)}, u32[]{:S(2)}, u32[]{:S(2)}) collective-permute-start(f32[32,768]{1,0:T(8,128)S(1)} %add_add_fusion), channel_id=1, source_target_pairs={{0,4},{1,5},{2,6},{3,7},{4,0},{5,1},{6,2},{7,3},{8,12},{9,13},{10,... | collective-permute-start | bytes 294920 | tf_op jit(solution)/shard_map/ppermute | solution.py:409
  112.2 4.9 %collective-permute-start.26 = (f32[32,768]{1,0:T(8,128)S(1)}, f32[32,768]{1,0:T(8,128)S(1)}, u32[]{:S(2)}, u32[]{:S(2)}) collective-permute-start(f32[32,768]{1,0:T(8,128)S(1)} %add_add_fusion), channel_id=1, source_target_pairs={{0,2},{1,3},{2,0},{3,1},{4,6},{5,7},{6,4},{7,5},{8,10},{9,11},{10,... | collective-permute-start | bytes 294920 | tf_op jit(solution)/shard_map/ppermute | solution.py:409
  (9 other events, 61.3 us)

commit v2 on v1

--- a/solution.py
+++ b/solution.py
@@ -310,13 +310,18 @@
 
 def carry_slots(plan, scale, odd, slots, inverse, basis, matrix, q, stages, outs, sems):
     jobs = []
+    triples = []
+    for m in range(2):
+        term = jnp.concatenate([slots[j, :, plan.part_span(m)] for j in range(plan.half)], axis=1)
+        term = dot32(inverse[m], term, NN) * scale
+        high, low = split(term)
+        triples.append(jnp.concatenate([high, low, high], axis=0))
+        for j in range(plan.half):
+            q[j, :, plan.part_span(m)] = term[:, j * plan.part[m] : (j + 1) * plan.part[m]]
     for j in range(plan.half):
         chunk = chunk_of(2 * j + odd)
         for m, (h, l) in enumerate((matrix[:2], matrix[2:])):
-            span = plan.part_span(m)
-            q[j, :, span] = dot32(inverse[m], slots[j, :, span], NN) * scale
-            high, low = split(q[j, :, span])
-            triple = jnp.concatenate([high, low, high], axis=0)
+            triple = triples[m][:, j * plan.part[m] : (j + 1) * plan.part[m]]
             at = plan.columns(m, chunk)
             for r in range(0, plan.rows[m], 2 * LANES):
                 rows = pl.ds(r, min(2 * LANES, plan.rows[m] - r))
@@ -409,8 +414,17 @@
     return lax.ppermute(x, axis, [(i, i ^ offset) for i in range(lax.axis_size(axis))])
 
 
+def turned(x, axis, offset):
+    size = lax.axis_size(axis)
+    return lax.ppermute(x, axis, [(i, (i + offset) % size) for i in range(size)])
+
+
 def exchanged(x, axis):
-    return [x] + [swapped(x, axis, k) for k in range(1, lax.axis_size(axis))]
+    size = lax.axis_size(axis)
+    terms = [x]
+    for k in range(1, size):
+        terms.append(turned(x, axis, k))
+    return terms
 
 
 def offsets(size):
@@ -435,11 +449,17 @@
 
 def gathered(odd, even):
     mine = even + swapped(odd, "shard", 1)
-    return tree([mine[0]] + [swapped(mine[j], "shard", 2 * j) for j in range(1, mine.shape[0])])
+    terms = [mine[0]]
+    for j in range(1, mine.shape[0]):
+        terms.append(swapped(mine[j], "shard", 2 * j))
+    return tree(terms)
 
 
 def spread(share, half):
-    return jnp.stack([share] + [swapped(share, "shard", 2 * j) for j in range(1, half)])
+    terms = [share]
+    for j in range(1, half):
+        terms.append(swapped(share, "shard", 2 * j))
+    return jnp.stack(terms)
 
 
 def compress(ag, ae, wa, fg, fe, wf):

time: 127 us -> 125 us (0.984)
    ppermute x30 -> x24, waiting for transfers between devices: 46.2 us -> 36.8 us  [swapped(): lax.ppermute(x, axis, [(i, i ^ offset) for i in range(lax.axis_size(axis))])]
    ppermute x0 -> x6, waiting for transfers between devices: none -> 8.65 us  [turned(): lax.ppermute(x, axis, [(i, (i + offset) % size) for i in range(size)])]
    ppermute x30 -> x24, starting transfers between devices: 38.8 us -> 31 us  [swapped(): lax.ppermute(x, axis, [(i, i ^ offset) for i in range(lax.axis_size(axis))])]
    ppermute x0 -> x6, starting transfers between devices: none -> 7.74 us  [turned(): lax.ppermute(x, axis, [(i, (i + offset) % size) for i in range(size)])]
where the time goes in v2:
time: 125 us
  waiting for transfers between devices  45.4 us (36%)
  Pallas kernels  39.4 us (32%)
  starting transfers between devices  38.8 us (31%)
    ppermute x24, waiting for transfers between devices, swapped(): lax.ppermute(x, axis, [(i, i ^ offset) for i in range(lax.axis_size(axis))])  36.8 us
    ppermute x24, starting transfers between devices, swapped(): lax.ppermute(x, axis, [(i, i ^ offset) for i in range(lax.axis_size(axis))])  31 us
    pallas_call x1, Pallas kernels, load(): pl.pallas_call(functools.partial(stream_kernel, plan, m), out_shape=outs,...  9.03 us
    ppermute x6, waiting for transfers between devices, turned(): lax.ppermute(x, axis, [(i, (i + offset) % size) for i in range(size)])  8.65 us
    ppermute x6, starting transfers between devices, turned(): lax.ppermute(x, axis, [(i, (i + offset) % size) for i in range(size)])  7.74 us
    pallas_call x6, Pallas kernels, call(): pl.pallas_call(kernel, out_shape=outs, in_specs=[VMEM] * len(operands), o...  7.29 us
    pallas_call x2, Pallas kernels, factor(): pl.pallas_call(functools.partial(factor_kernel, plan.rank), out_shape=jax...  5.86 us
    pallas_call x4, Pallas kernels, call(): pl.pallas_call(functools.partial(left_kernel, plan, m, parity), out_shape...  5.07 us
  transfers between devices with their start and end apart: 30, of which 23 were waited for; matrix products, arithmetic and copies ran while one was open for 0% of the time, Pallas kernels for 18%

profile of v2, /device:TPU:0, one launch (start us, length us, event | category | flops | bytes accessed | tf_op | source)
XLA Modules:
  0.0 125.1 jit_solution(4537941581372007992)
XLA Ops:
  0.7 9.0 %stream.1 = (bf16[992,2048]{1,0:T(8,128)(2,1)S(1)}, bf16[992,2048]{1,0:T(8,128)(2,1)S(1)}, f32[32,1024]{1,0:T(8,128)S(1)}) custom-call(f32[1,992,2048]{2,1,0:T(8,128)} %grad.3, f32[1,992,2048]{2,1,0:T(8,128)} %error.3, f32[32,2048]{1,0:T(8,128)} %warm.3), custom_call_target="tpu_custom_call" | custom-call | bytes 21000000 | tf_op jit(solution)/shard_map/stream/pallas_call | solution.py:160
  9.7 5.1 %collective-permute-start.2 = (f32[32,1024]{1,0:T(8,128)S(1)}, f32[32,1024]{1,0:T(8,128)S(1)}, u32[]{:S(2)}, u32[]{:S(2)}) collective-permute-start(f32[32,1024]{1,0:T(8,128)S(1)} %get-tuple-element.30), channel_id=1, source_target_pairs={{0,24},{8,16},{16,8},{24,0},{1,25},{9,17},{17,9},{25,1},{2,26},{10... | collective-permute-start | bytes 393224 | tf_op jit(solution)/shard_map/ppermute | solution.py:414
  14.9 3.0 %hold.1 = (bf16[496,4096]{1,0:T(8,128)(2,1)S(1)}, bf16[496,4096]{1,0:T(8,128)(2,1)S(1)}, f32[32,512]{1,0:T(8,128)S(1)}) custom-call(f32[1,496,3968]{2,1,0:T(8,128)S(1)} %copy-done, f32[1,496,3968]{2,1,0:T(8,128)S(1)} %copy-done.1, f32[32,3968]{1,0:T(8,128)S(1)} %copy-done.2), custom_call_target="tpu_custom_call" | custom-call | bytes 12000000 | tf_op jit(solution)/shard_map/hold/pallas_call | solution.py:149
  18.5 2.5 %collective-permute-start.3 = (f32[32,1024]{1,0:T(8,128)S(1)}, f32[32,1024]{1,0:T(8,128)S(1)}, u32[]{:S(2)}, u32[]{:S(2)}) collective-permute-start(f32[32,1024]{1,0:T(8,128)S(1)} %add.55.refs_0_), channel_id=1, source_target_pairs={{0,8},{8,0},{16,24},{24,16},{1,9},{9,1},{17,25},{25,17},{2,10},{10... | collective-permute-start | bytes 393224 | tf_op jit(solution)/shard_map/ppermute | solution.py:414
  21.0 4.2 %collective-permute-done = f32[32,512]{1,0:T(8,128)S(1)} collective-permute-done((f32[32,512]{1,0:T(8,128)S(1)}, f32[32,512]{1,0:T(8,128)S(1)}, u32[]{:S(2)}, u32[]{:S(2)}) %collective-permute-start) | collective-permute-done | bytes 65568 | tf_op jit(solution)/shard_map/ppermute | solution.py:414
  25.3 2.7 %collective-permute-start.1 = (f32[32,512]{1,0:T(8,128)S(1)}, f32[32,512]{1,0:T(8,128)S(1)}, u32[]{:S(2)}, u32[]{:S(2)}) collective-permute-start(f32[32,512]{1,0:T(8,128)S(1)} %add.54.refs_0_), channel_id=1, source_target_pairs={{0,24},{8,16},{16,8},{24,0},{1,25},{9,17},{17,9},{25,1},{2,26},{10... | collective-permute-start | bytes 196616 | tf_op jit(solution)/shard_map/ppermute | solution.py:414
  34.2 2.5 %collective-permute-start.7 = (f32[32,896]{1,0:T(8,128)S(1)}, f32[32,896]{1,0:T(8,128)S(1)}, u32[]{:S(2)}, u32[]{:S(2)}) collective-permute-start(f32[32,896]{1,0:T(8,128)S(1)} %get-tuple-element.57), channel_id=1, source_target_pairs={{0,6},{1,7},{2,4},{3,5},{4,2},{5,3},{6,0},{7,1},{8,14},{9,15},{10,... | collective-permute-start | bytes 344072 | tf_op jit(solution)/shard_map/ppermute | solution.py:414
  37.7 3.4 %collective-permute-done.7 = f32[32,896]{1,0:T(8,128)S(1)} collective-permute-done((f32[32,896]{1,0:T(8,128)S(1)}, f32[32,896]{1,0:T(8,128)S(1)}, u32[]{:S(2)}, u32[]{:S(2)}) %collective-permute-start.7) | collective-permute-done | bytes 114720 | tf_op jit(solution)/shard_map/ppermute | solution.py:414
  43.0 3.8 %collective-permute-start.10 = (f32[32,768]{1,0:T(8,128)S(1)}, f32[32,768]{1,0:T(8,128)S(1)}, u32[]{:S(2)}, u32[]{:S(2)}) collective-permute-start(f32[32,768]{1,0:T(8,128)S(1)} %slice.52), channel_id=1, source_target_pairs={{0,24},{8,0},{16,8},{24,16},{1,25},{9,1},{17,9},{25,17},{2,26},{10... | collective-permute-start | bytes 294920 | tf_op jit(solution)/shard_map/ppermute | solution.py:419
  46.8 2.9 %factor.2.refs_2_ = f32[2,32,32]{2,1,0:T(8,128)S(1)} custom-call(f32[32,128]{1,0:T(8,128)S(1)} %slice.53.gram), custom_call_target="tpu_custom_call" | custom-call | bytes 9000000 | tf_op jit(solution)/shard_map/factor/pallas_call | solution.py:300
  50.4 4.1 %collective-permute-done.8 = f32[32,768]{1,0:T(8,128)S(1)} collective-permute-done((f32[32,768]{1,0:T(8,128)S(1)}, f32[32,768]{1,0:T(8,128)S(1)}, u32[]{:S(2)}, u32[]{:S(2)}) %collective-permute-start.8) | collective-permute-done | bytes 98336 | tf_op jit(solution)/shard_map/ppermute | solution.py:419
  54.5 3.0 %collective-permute-start.13 = (f32[32,768]{1,0:T(8,128)S(1)}, f32[32,768]{1,0:T(8,128)S(1)}, u32[]{:S(2)}, u32[]{:S(2)}) collective-permute-start(f32[32,768]{1,0:T(8,128)S(1)} %add_add_fusion.1), channel_id=1, source_target_pairs={{0,6},{1,7},{2,4},{3,5},{4,2},{5,3},{6,0},{7,1},{8,14},{9,15},{10,... | collective-permute-start | bytes 294920 | tf_op jit(solution)/shard_map/ppermute | solution.py:414
  58.2 2.1 %collective-permute-done.13 = f32[32,768]{1,0:T(8,128)S(1)} collective-permute-done((f32[32,768]{1,0:T(8,128)S(1)}, f32[32,768]{1,0:T(8,128)S(1)}, u32[]{:S(2)}, u32[]{:S(2)}) %collective-permute-start.13) | collective-permute-done | bytes 98336 | tf_op jit(solution)/shard_map/ppermute | solution.py:414
  70.0 2.8 %collective-permute-done.17 = f32[32,1024]{1,0:T(8,128)S(1)} collective-permute-done((f32[32,1024]{1,0:T(8,128)S(1)}, f32[32,1024]{1,0:T(8,128)S(1)}, u32[]{:S(2)}, u32[]{:S(2)}) %collective-permute-start.17) | collective-permute-done | bytes 131104 | tf_op jit(solution)/shard_map/ppermute | solution.py:414
  75.0 4.1 %collective-permute-done.15 = f32[32,512]{1,0:T(8,128)S(1)} collective-permute-done((f32[32,512]{1,0:T(8,128)S(1)}, f32[32,512]{1,0:T(8,128)S(1)}, u32[]{:S(2)}, u32[]{:S(2)}) %collective-permute-start.15) | collective-permute-done | bytes 65568 | tf_op jit(solution)/shard_map/ppermute | solution.py:414
  79.0 2.1 %collective-permute-start.16 = (f32[32,512]{1,0:T(8,128)S(1)}, f32[32,512]{1,0:T(8,128)S(1)}, u32[]{:S(2)}, u32[]{:S(2)}) collective-permute-start(f32[32,512]{1,0:T(8,128)S(1)} %add.63.refs_0_), channel_id=1, source_target_pairs={{0,24},{8,16},{16,8},{24,0},{1,25},{9,17},{17,9},{25,1},{2,26},{10... | collective-permute-start | bytes 196616 | tf_op jit(solution)/shard_map/ppermute | solution.py:414
  82.9 2.3 %collective-permute-done.16.refs_1_ = f32[32,512]{1,0:T(8,128)S(1)} collective-permute-done((f32[32,512]{1,0:T(8,128)S(1)}, f32[32,512]{1,0:T(8,128)S(1)}, u32[]{:S(2)}, u32[]{:S(2)}) %collective-permute-start.16) | collective-permute-done | bytes 65568 | tf_op jit(solution)/shard_map/ppermute | solution.py:414
  91.7 3.4 %collective-permute-done.22 = f32[32,896]{1,0:T(8,128)S(1)} collective-permute-done((f32[32,896]{1,0:T(8,128)S(1)}, f32[32,896]{1,0:T(8,128)S(1)}, u32[]{:S(2)}, u32[]{:S(2)}) %collective-permute-start.22) | collective-permute-done | bytes 114720 | tf_op jit(solution)/shard_map/ppermute | solution.py:414
  97.2 3.8 %collective-permute-start.25 = (f32[32,768]{1,0:T(8,128)S(1)}, f32[32,768]{1,0:T(8,128)S(1)}, u32[]{:S(2)}, u32[]{:S(2)}) collective-permute-start(f32[32,768]{1,0:T(8,128)S(1)} %slice.58), channel_id=1, source_target_pairs={{0,24},{8,0},{16,8},{24,16},{1,25},{9,1},{17,9},{25,17},{2,26},{10... | collective-permute-start | bytes 294920 | tf_op jit(solution)/shard_map/ppermute | solution.py:419
  101.0 2.9 %factor.3.inverse = f32[2,32,32]{2,1,0:T(8,128)S(1)} custom-call(f32[32,128]{1,0:T(8,128)S(1)} %slice.59.gram), custom_call_target="tpu_custom_call" | custom-call | bytes 9000000 | tf_op jit(solution)/shard_map/factor/pallas_call | solution.py:300
  104.7 3.5 %collective-permute-done.23 = f32[32,768]{1,0:T(8,128)S(1)} collective-permute-done((f32[32,768]{1,0:T(8,128)S(1)}, f32[32,768]{1,0:T(8,128)S(1)}, u32[]{:S(2)}, u32[]{:S(2)}) %collective-permute-start.23) | collective-permute-done | bytes 98336 | tf_op jit(solution)/shard_map/ppermute | solution.py:419
  111.8 2.9 %collective-permute-done.28 = f32[32,768]{1,0:T(8,128)S(1)} collective-permute-done((f32[32,768]{1,0:T(8,128)S(1)}, f32[32,768]{1,0:T(8,128)S(1)}, u32[]{:S(2)}, u32[]{:S(2)}) %collective-permute-start.28) | collective-permute-done | bytes 98336 | tf_op jit(solution)/shard_map/ppermute | solution.py:414
  116.2 3.9 %carry_first.1 = (f32[1,496,3968]{2,1,0:T(8,128)}, f32[1,992,2048]{2,1,0:T(8,128)}, f32[4,32,768]{2,1,0:T(8,128)S(1)}) custom-call(f32[4,32,768]{2,1,0:T(8,128)S(1)} %pad_maximum_fusion.1.slots, f32[2,32,32]{2,1,0:T(8,128)S(1)} %factor.3.inverse, bf16[1536,96]{1,0:T(8,128)(2,1)S(1)} %basis.1, ...), custom_call_target="tpu_custom_call" | custom-call | bytes 12000000 | tf_op jit(solution)/shard_map/carry_first/pallas_call | solution.py:390
  120.1 4.8 %carry_second.1 = (f32[1,496,3968]{2,1,0:T(8,128)}, f32[1,992,2048]{2,1,0:T(8,128)}, f32[32,3968]{1,0:T(8,128)}, f32[32,2048]{1,0:T(8,128)}) custom-call(f32[4,32,768]{2,1,0:T(8,128)S(1)} %collective-permute-done.29.slots, f32[2,32,32]{2,1,0:T(8,128)S(1)} %factor.3.inverse, ...), custom_call_target="tpu_custom_call", output_to_operand_aliasing={{0}: (4, {}), {1}: (5, {})} | custom-call | bytes 12000000 | tf_op jit(solution)/shard_map/carry_second/pallas_call | solution.py:400
  (77 shorter events, 39.1 us)
Async XLA Ops:
  9.7 8.7 %collective-permute-start.2 = (f32[32,1024]{1,0:T(8,128)S(1)}, f32[32,1024]{1,0:T(8,128)S(1)}, u32[]{:S(2)}, u32[]{:S(2)}) collective-permute-start(f32[32,1024]{1,0:T(8,128)S(1)} %get-tuple-element.30), channel_id=1, source_target_pairs={{0,24},{8,16},{16,8},{24,0},{1,25},{9,17},{17,9},{25,1},{2,26},{10... | collective-permute-start | bytes 393224 | tf_op jit(solution)/shard_map/ppermute | solution.py:414
  18.5 9.5 %collective-permute-start.3 = (f32[32,1024]{1,0:T(8,128)S(1)}, f32[32,1024]{1,0:T(8,128)S(1)}, u32[]{:S(2)}, u32[]{:S(2)}) collective-permute-start(f32[32,1024]{1,0:T(8,128)S(1)} %add.55.refs_0_), channel_id=1, source_target_pairs={{0,8},{8,0},{16,24},{24,16},{1,9},{9,1},{17,25},{25,17},{2,10},{10... | collective-permute-start | bytes 393224 | tf_op jit(solution)/shard_map/ppermute | solution.py:414
  25.3 6.2 %collective-permute-start.1 = (f32[32,512]{1,0:T(8,128)S(1)}, f32[32,512]{1,0:T(8,128)S(1)}, u32[]{:S(2)}, u32[]{:S(2)}) collective-permute-start(f32[32,512]{1,0:T(8,128)S(1)} %add.54.refs_0_), channel_id=1, source_target_pairs={{0,24},{8,16},{16,8},{24,0},{1,25},{9,17},{17,9},{25,1},{2,26},{10... | collective-permute-start | bytes 196616 | tf_op jit(solution)/shard_map/ppermute | solution.py:414
  34.2 7.0 %collective-permute-start.7 = (f32[32,896]{1,0:T(8,128)S(1)}, f32[32,896]{1,0:T(8,128)S(1)}, u32[]{:S(2)}, u32[]{:S(2)}) collective-permute-start(f32[32,896]{1,0:T(8,128)S(1)} %get-tuple-element.57), channel_id=1, source_target_pairs={{0,6},{1,7},{2,4},{3,5},{4,2},{5,3},{6,0},{7,1},{8,14},{9,15},{10,... | collective-permute-start | bytes 344072 | tf_op jit(solution)/shard_map/ppermute | solution.py:414
  36.7 6.2 %collective-permute-start.6 = (f32[32,896]{1,0:T(8,128)S(1)}, f32[32,896]{1,0:T(8,128)S(1)}, u32[]{:S(2)}, u32[]{:S(2)}) collective-permute-start(f32[32,896]{1,0:T(8,128)S(1)} %get-tuple-element.58), channel_id=1, source_target_pairs={{0,2},{1,3},{2,0},{3,1},{4,6},{5,7},{6,4},{7,5},{8,10},{9,11},{10,... | collective-permute-start | bytes 344072 | tf_op jit(solution)/shard_map/ppermute | solution.py:414
  37.2 5.6 %collective-permute-start.5 = (f32[32,896]{1,0:T(8,128)S(1)}, f32[32,896]{1,0:T(8,128)S(1)}, u32[]{:S(2)}, u32[]{:S(2)}) collective-permute-start(f32[32,896]{1,0:T(8,128)S(1)} %get-tuple-element.59), channel_id=1, source_target_pairs={{0,4},{1,5},{2,6},{3,7},{4,0},{5,1},{6,2},{7,3},{8,12},{9,13},{10,... | collective-permute-start | bytes 344072 | tf_op jit(solution)/shard_map/ppermute | solution.py:414
  42.9 7.5 %collective-permute-start.9 = (f32[32,768]{1,0:T(8,128)S(1)}, f32[32,768]{1,0:T(8,128)S(1)}, u32[]{:S(2)}, u32[]{:S(2)}) collective-permute-start(f32[32,768]{1,0:T(8,128)S(1)} %slice.52), channel_id=1, source_target_pairs={{0,8},{8,16},{16,24},{24,0},{1,9},{9,17},{17,25},{25,1},{2,10},{10... | collective-permute-start | bytes 294920 | tf_op jit(solution)/shard_map/ppermute | solution.py:419
  43.0 7.5 %collective-permute-start.10 = (f32[32,768]{1,0:T(8,128)S(1)}, f32[32,768]{1,0:T(8,128)S(1)}, u32[]{:S(2)}, u32[]{:S(2)}) collective-permute-start(f32[32,768]{1,0:T(8,128)S(1)} %slice.52), channel_id=1, source_target_pairs={{0,24},{8,0},{16,8},{24,16},{1,25},{9,1},{17,9},{25,17},{2,26},{10... | collective-permute-start | bytes 294920 | tf_op jit(solution)/shard_map/ppermute | solution.py:419
  46.8 7.7 %collective-permute-start.8 = (f32[32,768]{1,0:T(8,128)S(1)}, f32[32,768]{1,0:T(8,128)S(1)}, u32[]{:S(2)}, u32[]{:S(2)}) collective-permute-start(f32[32,768]{1,0:T(8,128)S(1)} %slice.52), channel_id=1, source_target_pairs={{0,16},{8,24},{16,0},{24,8},{1,17},{9,25},{17,1},{25,9},{2,18},{10... | collective-permute-start | bytes 294920 | tf_op jit(solution)/shard_map/ppermute | solution.py:419
  54.5 5.7 %collective-permute-start.13 = (f32[32,768]{1,0:T(8,128)S(1)}, f32[32,768]{1,0:T(8,128)S(1)}, u32[]{:S(2)}, u32[]{:S(2)}) collective-permute-start(f32[32,768]{1,0:T(8,128)S(1)} %add_add_fusion.1), channel_id=1, source_target_pairs={{0,6},{1,7},{2,4},{3,5},{4,2},{5,3},{6,0},{7,1},{8,14},{9,15},{10,... | collective-permute-start | bytes 294920 | tf_op jit(solution)/shard_map/ppermute | solution.py:414
  57.6 4.8 %collective-permute-start.11 = (f32[32,768]{1,0:T(8,128)S(1)}, f32[32,768]{1,0:T(8,128)S(1)}, u32[]{:S(2)}, u32[]{:S(2)}) collective-permute-start(f32[32,768]{1,0:T(8,128)S(1)} %add_add_fusion.1), channel_id=1, source_target_pairs={{0,2},{1,3},{2,0},{3,1},{4,6},{5,7},{6,4},{7,5},{8,10},{9,11},{10,... | collective-permute-start | bytes 294920 | tf_op jit(solution)/shard_map/ppermute | solution.py:414
  65.5 7.4 %collective-permute-start.17 = (f32[32,1024]{1,0:T(8,128)S(1)}, f32[32,1024]{1,0:T(8,128)S(1)}, u32[]{:S(2)}, u32[]{:S(2)}) collective-permute-start(f32[32,1024]{1,0:T(8,128)S(1)} %shard_map.99), channel_id=1, source_target_pairs={{0,24},{8,16},{16,8},{24,0},{1,25},{9,17},{17,9},{25,1},{2,26},{10... | collective-permute-start | bytes 393224 | tf_op jit(solution)/shard_map/ppermute | solution.py:414
  72.9 8.2 %collective-permute-start.18 = (f32[32,1024]{1,0:T(8,128)S(1)}, f32[32,1024]{1,0:T(8,128)S(1)}, u32[]{:S(2)}, u32[]{:S(2)}) collective-permute-start(f32[32,1024]{1,0:T(8,128)S(1)} %add.64.refs_0_), channel_id=1, source_target_pairs={{0,8},{8,0},{16,24},{24,16},{1,9},{9,1},{17,25},{25,17},{2,10},{10... | collective-permute-start | bytes 393224 | tf_op jit(solution)/shard_map/ppermute | solution.py:414
  72.9 6.1 %collective-permute-start.15 = (f32[32,512]{1,0:T(8,128)S(1)}, f32[32,512]{1,0:T(8,128)S(1)}, u32[]{:S(2)}, u32[]{:S(2)}) collective-permute-start(f32[32,512]{1,0:T(8,128)S(1)} %shard_map.97), channel_id=1, source_target_pairs={{0,8},{8,0},{16,24},{24,16},{1,9},{9,1},{17,25},{25,17},{2,10},{10... | collective-permute-start | bytes 196616 | tf_op jit(solution)/shard_map/ppermute | solution.py:414
  79.0 6.1 %collective-permute-start.16 = (f32[32,512]{1,0:T(8,128)S(1)}, f32[32,512]{1,0:T(8,128)S(1)}, u32[]{:S(2)}, u32[]{:S(2)}) collective-permute-start(f32[32,512]{1,0:T(8,128)S(1)} %add.63.refs_0_), channel_id=1, source_target_pairs={{0,24},{8,16},{16,8},{24,0},{1,25},{9,17},{17,9},{25,1},{2,26},{10... | collective-permute-start | bytes 196616 | tf_op jit(solution)/shard_map/ppermute | solution.py:414
  88.1 7.0 %collective-permute-start.22 = (f32[32,896]{1,0:T(8,128)S(1)}, f32[32,896]{1,0:T(8,128)S(1)}, u32[]{:S(2)}, u32[]{:S(2)}) collective-permute-start(f32[32,896]{1,0:T(8,128)S(1)} %get-tuple-element.54), channel_id=1, source_target_pairs={{0,6},{1,7},{2,4},{3,5},{4,2},{5,3},{6,0},{7,1},{8,14},{9,15},{10,... | collective-permute-start | bytes 344072 | tf_op jit(solution)/shard_map/ppermute | solution.py:414
  90.0 7.1 %collective-permute-start.21 = (f32[32,896]{1,0:T(8,128)S(1)}, f32[32,896]{1,0:T(8,128)S(1)}, u32[]{:S(2)}, u32[]{:S(2)}) collective-permute-start(f32[32,896]{1,0:T(8,128)S(1)} %get-tuple-element.55), channel_id=1, source_target_pairs={{0,2},{1,3},{2,0},{3,1},{4,6},{5,7},{6,4},{7,5},{8,10},{9,11},{10,... | collective-permute-start | bytes 344072 | tf_op jit(solution)/shard_map/ppermute | solution.py:414
  91.5 5.6 %collective-permute-start.20 = (f32[32,896]{1,0:T(8,128)S(1)}, f32[32,896]{1,0:T(8,128)S(1)}, u32[]{:S(2)}, u32[]{:S(2)}) collective-permute-start(f32[32,896]{1,0:T(8,128)S(1)} %get-tuple-element.56), channel_id=1, source_target_pairs={{0,4},{1,5},{2,6},{3,7},{4,0},{5,1},{6,2},{7,3},{8,12},{9,13},{10,... | collective-permute-start | bytes 344072 | tf_op jit(solution)/shard_map/ppermute | solution.py:414
  97.1 7.6 %collective-permute-start.24 = (f32[32,768]{1,0:T(8,128)S(1)}, f32[32,768]{1,0:T(8,128)S(1)}, u32[]{:S(2)}, u32[]{:S(2)}) collective-permute-start(f32[32,768]{1,0:T(8,128)S(1)} %slice.58), channel_id=1, source_target_pairs={{0,8},{8,16},{16,24},{24,0},{1,9},{9,17},{17,25},{25,1},{2,10},{10... | collective-permute-start | bytes 294920 | tf_op jit(solution)/shard_map/ppermute | solution.py:419
  97.2 7.6 %collective-permute-start.25 = (f32[32,768]{1,0:T(8,128)S(1)}, f32[32,768]{1,0:T(8,128)S(1)}, u32[]{:S(2)}, u32[]{:S(2)}) collective-permute-start(f32[32,768]{1,0:T(8,128)S(1)} %slice.58), channel_id=1, source_target_pairs={{0,24},{8,0},{16,8},{24,16},{1,25},{9,1},{17,9},{25,17},{2,26},{10... | collective-permute-start | bytes 294920 | tf_op jit(solution)/shard_map/ppermute | solution.py:419
  101.0 7.2 %collective-permute-start.23 = (f32[32,768]{1,0:T(8,128)S(1)}, f32[32,768]{1,0:T(8,128)S(1)}, u32[]{:S(2)}, u32[]{:S(2)}) collective-permute-start(f32[32,768]{1,0:T(8,128)S(1)} %slice.58), channel_id=1, source_target_pairs={{0,16},{8,24},{16,0},{24,8},{1,17},{9,25},{17,1},{25,9},{2,18},{10... | collective-permute-start | bytes 294920 | tf_op jit(solution)/shard_map/ppermute | solution.py:419
  108.2 6.5 %collective-permute-start.28 = (f32[32,768]{1,0:T(8,128)S(1)}, f32[32,768]{1,0:T(8,128)S(1)}, u32[]{:S(2)}, u32[]{:S(2)}) collective-permute-start(f32[32,768]{1,0:T(8,128)S(1)} %add_add_fusion), channel_id=1, source_target_pairs={{0,6},{1,7},{2,4},{3,5},{4,2},{5,3},{6,0},{7,1},{8,14},{9,15},{10,... | collective-permute-start | bytes 294920 | tf_op jit(solution)/shard_map/ppermute | solution.py:414
  109.9 5.8 %collective-permute-start.27 = (f32[32,768]{1,0:T(8,128)S(1)}, f32[32,768]{1,0:T(8,128)S(1)}, u32[]{:S(2)}, u32[]{:S(2)}) collective-permute-start(f32[32,768]{1,0:T(8,128)S(1)} %add_add_fusion), channel_id=1, source_target_pairs={{0,4},{1,5},{2,6},{3,7},{4,0},{5,1},{6,2},{7,3},{8,12},{9,13},{10,... | collective-permute-start | bytes 294920 | tf_op jit(solution)/shard_map/ppermute | solution.py:414
  111.2 4.8 %collective-permute-start.26 = (f32[32,768]{1,0:T(8,128)S(1)}, f32[32,768]{1,0:T(8,128)S(1)}, u32[]{:S(2)}, u32[]{:S(2)}) collective-permute-start(f32[32,768]{1,0:T(8,128)S(1)} %add_add_fusion), channel_id=1, source_target_pairs={{0,2},{1,3},{2,0},{3,1},{4,6},{5,7},{6,4},{7,5},{8,10},{9,11},{10,... | collective-permute-start | bytes 294920 | tf_op jit(solution)/shard_map/ppermute | solution.py:414
  (9 other events, 61.1 us)
